TPU v7x, 512 devices: a whole 4x8x8 slice. The times are simulated.
512 devices in a mesh: member: 8 (over y_hi, x), lat: 64 (over y_lo, z, core).
Axes of the slice: x: 4, y: 8 (y_hi: 2, y_lo: 4; y = y_hi * 4 + y_lo), z: 8, core: 2. Of those that a mesh axis runs over, the one named last changes fastest.
Arguments:
- atmosphere: float32 [2, 16, 8, 384, 1536], P(None, 'member', None, 'lat'), may hold values from -4 to 4
- ocean_state: float32 [2, 384, 1536], P(None, 'lat', 'member'), may hold values from -4 to 4
- viscosity: float32 [384, 1536], P('lat', 'member'), may hold values from 0.02 to 0.2
- sea_mask: int32 [384, 1536], P('lat'), may hold values 0 or 1
- parameter_index: int32 [16], P('member'), may hold values from 0 to 31
- parameter_table: float32 [32, 3], replicated, may hold values from 0.1 to 0.3
- level_mix: float32 [8, 8], replicated, may hold values from -0.5 to 0.5
Outputs:
- atmos_out: float32 [2, 16, 8, 384, 1536], P(None, 'member', None, 'lat')
- ocean_out: float32 [2, 384, 1536], P(None, 'lat', 'member')
All inputs are finite; a program needn't handle non-finite values. No bound on the sum of `sea_mask` on one device may be relied on, other than what follows from the above.
Results may differ from a plain program's by a relative error of at most 0.00011.
Values sent between devices are 32-bit elements; how exact they have to be, the bound alone decides.
A program may use at most 64 MiB of HBM per device.

v0:
```python
import jax
import jax.numpy as jnp
from jax import lax
from jax.sharding import PartitionSpec as P

ASTEPS = 3
OSTEPS = 2
COUPLE = 2


ADVECTION = 0.1
OCEAN_GAIN = 0.5
OCEAN_DIFFUSION = 0.15


def with_halo(block, sides, width, periodic):
    for axis, dim in sides:
        count = lax.axis_size(axis)
        forward = [(i, i + 1) for i in range(count - 1)]
        if periodic:
            forward.append((count - 1, 0))
        backward = [(target, source) for source, target in forward]
        low = lax.ppermute(
            lax.slice_in_dim(block, block.shape[dim] - width, None, axis=dim), axis, forward
        )
        high = lax.ppermute(lax.slice_in_dim(block, 0, width, axis=dim), axis, backward)
        block = jnp.concatenate([low, block, high], axis=dim)
    return block


def lookup(parameter_index, parameter_table):
    onehot = (
        parameter_index[:, None] == jnp.arange(parameter_table.shape[0], dtype=jnp.int32)[None, :]
    ).astype(jnp.float32)
    picked = jnp.dot(
        onehot, parameter_table, precision=lax.Precision.HIGHEST, preferred_element_type=jnp.float32
    )
    return (0.6 * picked[:, 0], 2.0 * jnp.transpose(picked[:, 1:3]))


def atmos_step(padded_rows, surface, diffusivity, exchange, level_mix):
    centre = padded_rows[:, :, :, 1:-1, :]
    northern = padded_rows[:, :, :, 2:, :]
    southern = padded_rows[:, :, :, :-2, :]
    eastern = jnp.roll(centre, -1, axis=4)
    western = jnp.roll(centre, 1, axis=4)
    laplace = eastern + western + northern + southern - 4.0 * centre
    zonal_wind = centre[1]
    advected = (
        centre
        - ADVECTION * zonal_wind[None] * (eastern - western) * 0.5
        + diffusivity[None, :, None, None, None] * laplace
    )
    mixed_state = advected + jnp.einsum(
        "kl,fmlrn->fmkrn", level_mix, advected, precision=lax.Precision.HIGHEST
    )
    bottom = mixed_state[:, :, 0] + exchange[:, :, None, None] * (
        surface[:, None] - mixed_state[:, :, 0]
    )
    return mixed_state.at[:, :, 0].set(bottom)


def atmos_window(atmos_state, surface, diffusivity, exchange, level_mix):
    for substep in range(ASTEPS):
        padded_rows = with_halo(atmos_state, (("lat", 3),), 1, False)
        atmos_state = atmos_step(padded_rows, surface, diffusivity, exchange, level_mix)
    return atmos_state


def ocean_step(ocean, forcing, ocean_rate, ocean_mask):
    padded_ocean = with_halo(ocean, (("lat", 1),), 1, False)
    columns = with_halo(ocean, (("member", 2),), 1, True)
    eastern = columns[:, :, 2:]
    western = columns[:, :, :-2]
    laplace = padded_ocean[:, 2:] + padded_ocean[:, :-2] + eastern + western - 4.0 * ocean
    return ocean + ocean_mask[None] * (OCEAN_GAIN * forcing + ocean_rate * laplace)


def body(atmosphere, ocean_state, viscosity, sea_mask, parameter_index, parameter_table, level_mix):
    local_members = atmosphere.shape[1]
    tile_width = ocean_state.shape[2]
    members = local_members * lax.axis_size("member")
    diffusivity, exchange = lookup(parameter_index, parameter_table)
    full_mask = sea_mask.astype(jnp.float32)
    tile_start = lax.axis_index("member") * tile_width
    ocean = ocean_state
    ocean_mask = lax.dynamic_slice_in_dim(full_mask, tile_start, tile_width, 1)
    ocean_rate = jnp.stack([jnp.full_like(viscosity, OCEAN_DIFFUSION), viscosity])
    atmos_state = atmosphere
    for coupling in range(COUPLE):
        surface = lax.all_gather(ocean, "member", axis=2, tiled=True)
        atmos_state = atmos_window(atmos_state, surface, diffusivity, exchange, level_mix)
        flux_terms = jnp.sum(
            exchange[:, :, None, None] * (atmos_state[:, :, 0] - surface[:, None]), axis=1
        )
        forcing = lax.psum_scatter(flux_terms, "member", scatter_dimension=2, tiled=True) / members
        for substep in range(OSTEPS):
            ocean = ocean_step(ocean, forcing, ocean_rate, ocean_mask)
    return (atmos_state, ocean)


def solution(mesh):
    return jax.shard_map(
        body,
        mesh=mesh,
        in_specs=(
            P(None, "member", None, "lat", None),
            P(None, "lat", "member"),
            P("lat", "member"),
            P("lat", None),
            P("member"),
            P(),
            P(),
        ),
        out_specs=(P(None, "member", None, "lat", None), P(None, "lat", "member")),
        check_vma=False,
    )
```

profile of v0, /device:TPU:48, one launch (start us, length us, event | category | flops | bytes accessed | tf_op | source)
XLA Modules:
  0.0 473.0 jit_solution(4835626749836713685)
XLA Ops:
  8.3 11.2 %collective-permute-start = (f32[2,2,8,1,1536]{4,2,3,1,0:T(8,128)S(1)}, f32[2,2,8,1,1536]{4,2,3,1,0:T(8,128)}, u32[]{:S(2)}, u32[]{:S(2)}) collective-permute-start(f32[2,2,8,1,1536]{4,2,3,1,0:T(8,128)S(1)} %get-tuple-element.118), channel_id=1, source_target_pairs={{1,0},{2,1},{3,2},{4,3},{5,4},{6,5},{7,6},{8,7},{9,8},{10,9},{11,1... | collective-permute-start | bytes 589832 | tf_op jit(solution)/shard_map/ppermute | solution.py:26
  19.5 1.9 collective-permute-start.1
  22.8 5.1 %collective-permute-start.10 = (f32[2,6,1]{2,1,0:T(8,128)}, f32[2,6,1]{2,1,0:T(8,128)}, u32[]{:S(2)}, u32[]{:S(2)}) collective-permute-start(f32[2,6,1]{2,1,0:T(8,128)} %get-tuple-element.132), channel_id=1, source_target_pairs={{64,0},{128,64},{192,128},{256,192},{320,256},{384,320},{448,384},... | collective-permute-start | bytes 152 | tf_op jit(solution)/shard_map/ppermute | solution.py:26
  27.9 1.9 collective-permute-start.11
  31.1 5.6 %collective-permute-start.8 = (f32[2,1,192]{2,1,0:T(1,128)}, f32[2,1,192]{2,1,0:T(1,128)}, u32[]{:S(2)}, u32[]{:S(2)}) collective-permute-start(f32[2,1,192]{2,1,0:T(1,128)} %copy.68), channel_id=1, source_target_pairs={{1,0},{2,1},{3,2},{4,3},{5,4},{6,5},{7,6},{8,7},{9,8},{10,9},{11,1... | collective-permute-start | bytes 4616 | tf_op jit(solution)/shard_map/ppermute | solution.py:26
  36.7 3.5 fusion.206
  42.3 50.8 %all_gather.6 = f32[2,6,1536]{1,0,2:T(2,128)S(1)} all-gather(f32[2,6,192]{1,0,2:T(2,128)S(1)} %copy.63), channel_id=1, replica_groups=mesh['member'=8,'lat'=64] {'member'}, dimensions={2}, use_global_device_ids=true | all-gather | bytes 82944 | tf_op jit(solution)/shard_map/all_gather | solution.py:91
  96.3 5.4 %fusion.5 = f32[2,2,8,6,1536]{4,2,3,1,0:T(8,128)S(1)} fusion(f32[2,2,8,6,1536]{4,2,3,1,0:T(8,128)S(1)} %copy-done.1, f32[2,2,8,1,1536]{4,2,3,1,0:T(8,128)} %collective-permute-done.1, f32[2,2,8,1,1536]{4,2,3,1,0:T(8,128)} %collective-permute-done, f32[2,2,8,6,1535]{4,2,3,1,0:T(8,128)} %get-tuple-element.115, f32[2,2,8,6,1]{4,2,3,1,0:T(8,128)S(1)} %get-tuple-element.117, ...), kind=kOutput, calls=%fused_computation.11 | convolution fusion | flops 37453824 | bytes 5701896 | tf_op jit(solution)/shard_map/kl,fmlrn->fmkrn/dot_general | solution.py:54
  103.4 1.9 collective-permute-start.2
  105.3 2.4 collective-permute-start.3
  108.5 5.9 %collective-permute-done.3 = f32[2,2,8,1,1536]{4,2,3,1,0:T(8,128)S(1)} collective-permute-done((f32[2,2,8,1,1536]{4,2,3,1,0:T(8,128)S(1)}, f32[2,2,8,1,1536]{4,2,3,1,0:T(8,128)S(1)}, u32[]{:S(2)}, u32[]{:S(2)}) %collective-permute-start.3) | collective-permute-done | bytes 196640 | tf_op jit(solution)/shard_map/ppermute | solution.py:23
  114.4 2.6 fusion.4
  118.8 1.9 collective-permute-start.4
  120.7 2.4 collective-permute-start.5
  123.9 1.9 collective-permute-start.9
  125.8 4.0 collective-permute-done.5
  129.8 2.6 fusion.3
  133.7 1.8 fusion.197
  138.3 1.8 reshape.255
  140.9 1.9 collective-permute-start.6
  142.8 82.0 %reduce-scatter.7.cloned.1.call-done = f32[192,12]{1,0:T(8,128)} async-done(((f32[1536,12]{1,0:T(8,128)}), f32[192,12]{1,0:T(8,128)}) %reduce-scatter.7.cloned.1.call-update) | async-done | bytes 9232
  226.0 1.9 collective-permute-start.7
  228.8 5.8 %collective-permute-start.12 = (f32[2,1,192]{2,1,0:T(1,128)S(1)}, f32[2,1,192]{2,1,0:T(1,128)S(1)}, u32[]{:S(2)}, u32[]{:S(2)}) collective-permute-start(f32[2,1,192]{2,1,0:T(1,128)S(1)} %get-tuple-element.128), channel_id=1, source_target_pairs={{1,0},{2,1},{3,2},{4,3},{5,4},{6,5},{7,6},{8,7},{9,8},{10,9},{11,1... | collective-permute-start | bytes 4616 | tf_op jit(solution)/shard_map/ppermute | solution.py:26
  234.6 1.9 collective-permute-start.13
  236.6 6.6 %collective-permute-start.14 = (f32[2,6,1]{2,1,0:T(8,128)S(1)}, f32[2,6,1]{2,1,0:T(8,128)S(1)}, u32[]{:S(2)}, u32[]{:S(2)}) collective-permute-start(f32[2,6,1]{2,1,0:T(8,128)S(1)} %get-tuple-element.130), channel_id=1, source_target_pairs={{64,0},{128,64},{192,128},{256,192},{320,256},{384,320},{448,384},... | collective-permute-start | bytes 152 | tf_op jit(solution)/shard_map/ppermute | solution.py:26
  244.5 2.1 collective-permute-start.15
  246.6 9.9 %collective-permute-done.15 = f32[2,6,1]{2,1,0:T(8,128)S(1)} collective-permute-done((f32[2,6,1]{2,1,0:T(8,128)S(1)}, f32[2,6,1]{2,1,0:T(8,128)S(1)}, u32[]{:S(2)}, u32[]{:S(2)}) %collective-permute-start.15) | collective-permute-done | bytes 80 | tf_op jit(solution)/shard_map/ppermute | solution.py:23
  256.8 51.3 %all_gather.7 = f32[2,6,1536]{1,0,2:T(2,128)S(1)} all-gather(f32[2,6,192]{1,0,2:T(2,128)S(1)} %copy.78), channel_id=1, replica_groups=mesh['member'=8,'lat'=64] {'member'}, dimensions={2}, use_global_device_ids=true | all-gather | bytes 82944 | tf_op jit(solution)/shard_map/all_gather | solution.py:91
  308.8 1.9 collective-permute-start.20
  310.8 2.4 collective-permute-start.21
  313.2 5.2 %fusion.2 = f32[2,2,8,6,1536]{4,2,3,1,0:T(8,128)S(1)} fusion(f32[2,2,8,6,1536]{4,2,3,1,0:T(8,128)S(1)} %scatter.24, f32[2,2,8,1,1536]{4,2,3,1,0:T(8,128)} %collective-permute-done.7, f32[2,2,8,1,1536]{4,2,3,1,0:T(8,128)} %collective-permute-done.6, f32[2,2,8,6,1535]{4,2,3,1,0:T(8,128)} %get-tuple-element.97, f32[2,2,8,6,1]{4,2,3,1,0:T(8,128)} %get-tuple-element.99, ...), kind=kOutput, calls=%fused_computation.5 | convolution fusion | flops 37453824 | bytes 5701896 | tf_op jit(solution)/shard_map/kl,fmlrn->fmkrn/dot_general | solution.py:54
  320.1 5.3 %collective-permute-start.16 = (f32[2,2,8,1,1536]{4,2,3,1,0:T(8,128)S(1)}, f32[2,2,8,1,1536]{4,2,3,1,0:T(8,128)S(1)}, u32[]{:S(2)}, u32[]{:S(2)}) collective-permute-start(f32[2,2,8,1,1536]{4,2,3,1,0:T(8,128)S(1)} %get-tuple-element.92), channel_id=1, source_target_pairs={{1,0},{2,1},{3,2},{4,3},{5,4},{6,5},{7,6},{8,7},{9,8},{10,9},{11,1... | collective-permute-start | bytes 589832 | tf_op jit(solution)/shard_map/ppermute | solution.py:26
  325.4 1.9 collective-permute-start.17
  328.5 5.9 %collective-permute-done.17 = f32[2,2,8,1,1536]{4,2,3,1,0:T(8,128)S(1)} collective-permute-done((f32[2,2,8,1,1536]{4,2,3,1,0:T(8,128)S(1)}, f32[2,2,8,1,1536]{4,2,3,1,0:T(8,128)S(1)}, u32[]{:S(2)}, u32[]{:S(2)}) %collective-permute-start.17) | collective-permute-done | bytes 196640 | tf_op jit(solution)/shard_map/ppermute | solution.py:23
  334.5 2.6 fusion.1
  338.8 1.9 collective-permute-start.18
  340.7 2.4 collective-permute-start.19
  343.9 5.9 %collective-permute-done.19 = f32[2,2,8,1,1536]{4,2,3,1,0:T(8,128)S(1)} collective-permute-done((f32[2,2,8,1,1536]{4,2,3,1,0:T(8,128)S(1)}, f32[2,2,8,1,1536]{4,2,3,1,0:T(8,128)S(1)}, u32[]{:S(2)}, u32[]{:S(2)}) %collective-permute-start.19) | collective-permute-done | bytes 196640 | tf_op jit(solution)/shard_map/ppermute | solution.py:23
  349.8 2.6 fusion
  354.0 1.8 reshape.257
  355.9 1.9 collective-permute-start.22
  357.8 3.9 collective-permute-start.23
  362.6 76.5 %reduce-scatter.9.cloned.1.call-done = f32[192,12]{1,0:T(8,128)} async-done(((f32[1536,12]{1,0:T(8,128)}), f32[192,12]{1,0:T(8,128)}) %reduce-scatter.9.cloned.1.call-update) | async-done | bytes 9232
  440.4 3.5 collective-permute-start.24
  443.9 1.9 collective-permute-start.25
  445.9 8.0 %collective-permute-start.26 = (f32[2,6,1]{2,1,0:T(8,128)S(1)}, f32[2,6,1]{2,1,0:T(8,128)S(1)}, u32[]{:S(2)}, u32[]{:S(2)}) collective-permute-start(f32[2,6,1]{2,1,0:T(8,128)S(1)} %get-tuple-element.122), channel_id=1, source_target_pairs={{64,0},{128,64},{192,128},{256,192},{320,256},{384,320},{448,384},... | collective-permute-start | bytes 152 | tf_op jit(solution)/shard_map/ppermute | solution.py:26
  453.9 1.9 collective-permute-start.27
  455.9 9.6 %collective-permute-done.27 = f32[2,6,1]{2,1,0:T(8,128)S(1)} collective-permute-done((f32[2,6,1]{2,1,0:T(8,128)S(1)}, f32[2,6,1]{2,1,0:T(8,128)S(1)}, u32[]{:S(2)}, u32[]{:S(2)}) %collective-permute-start.27) | collective-permute-done | bytes 80 | tf_op jit(solution)/shard_map/ppermute | solution.py:23
  (127 shorter events, 33.1 us)
Async XLA Ops:
  7.2 89.1 %copy-start = (f32[8,8]{1,0:T(8,128)S(1)}, f32[8,8]{1,0:T(8,128)}, u32[]{:S(2)}) copy-start(f32[8,8]{1,0:T(8,128)} %param.25) | copy-start | bytes 772
  7.2 217.7 %reduce-scatter.7.cloned.1.call-start = ((), (), s32[]{:S(2)}) async-start(), calls=%async_computation.2 | async-start | bytes 884736
  8.3 87.9 %collective-permute-start = (f32[2,2,8,1,1536]{4,2,3,1,0:T(8,128)S(1)}, f32[2,2,8,1,1536]{4,2,3,1,0:T(8,128)}, u32[]{:S(2)}, u32[]{:S(2)}) collective-permute-start(f32[2,2,8,1,1536]{4,2,3,1,0:T(8,128)S(1)} %get-tuple-element.118), channel_id=1, source_target_pairs={{1,0},{2,1},{3,2},{4,3},{5,4},{6,5},{7,6},{8,7},{9,8},{10,9},{11,1... | collective-permute-start | bytes 589832 | tf_op jit(solution)/shard_map/ppermute | solution.py:26
  19.5 76.8 %collective-permute-start.1 = (f32[2,2,8,1,1536]{4,2,3,1,0:T(8,128)S(1)}, f32[2,2,8,1,1536]{4,2,3,1,0:T(8,128)}, u32[]{:S(2)}, u32[]{:S(2)}) collective-permute-start(f32[2,2,8,1,1536]{4,2,3,1,0:T(8,128)S(1)} %get-tuple-element.119), channel_id=1, source_target_pairs={{0,1},{1,2},{2,3},{3,4},{4,5},{5,6},{6,7},{7,8},{8,9},{9,10},{10,1... | collective-permute-start | bytes 589832 | tf_op jit(solution)/shard_map/ppermute | solution.py:23
  22.1 8.4 %copy-start.6 = (f32[2,6,192]{2,1,0:T(8,128)}, f32[2,6,192]{2,1,0:T(8,128)S(1)}, u32[]{:S(2)}) copy-start(f32[2,6,192]{2,1,0:T(8,128)S(1)} %copy.77) | copy-start | bytes 27652
  22.8 203.2 %collective-permute-start.10 = (f32[2,6,1]{2,1,0:T(8,128)}, f32[2,6,1]{2,1,0:T(8,128)}, u32[]{:S(2)}, u32[]{:S(2)}) collective-permute-start(f32[2,6,1]{2,1,0:T(8,128)} %get-tuple-element.132), channel_id=1, source_target_pairs={{64,0},{128,64},{192,128},{256,192},{320,256},{384,320},{448,384},... | collective-permute-start | bytes 152 | tf_op jit(solution)/shard_map/ppermute | solution.py:26
  27.9 200.1 %collective-permute-start.11 = (f32[2,6,1]{2,1,0:T(8,128)}, f32[2,6,1]{2,1,0:T(8,128)}, u32[]{:S(2)}, u32[]{:S(2)}) collective-permute-start(f32[2,6,1]{2,1,0:T(8,128)} %get-tuple-element.133), channel_id=1, source_target_pairs={{0,64},{64,128},{128,192},{192,256},{256,320},{320,384},{384,448},... | collective-permute-start | bytes 152 | tf_op jit(solution)/shard_map/ppermute | solution.py:23
  31.1 9.1 %copy-start.1 = (f32[2,2,8,6,1536]{4,2,3,1,0:T(8,128)S(1)}, f32[2,2,8,6,1536]{4,2,3,1,0:T(8,128)}, u32[]{:S(2)}) copy-start(f32[2,2,8,6,1536]{4,2,3,1,0:T(8,128)} %param.19) | copy-start | bytes 3538948
  31.1 10.0 %copy-start.12 = (f32[32,3]{0,1:T(4,128)S(1)}, f32[32,3]{0,1:T(4,128)}, u32[]{:S(2)}) copy-start(f32[32,3]{0,1:T(4,128)} %param.24) | copy-start | bytes 1156
  31.1 10.0 %copy-start.13 = (s32[2]{0:T(128)S(1)}, s32[2]{0:T(128)}, u32[]{:S(2)}) copy-start(s32[2]{0:T(128)} %param.23) | copy-start | bytes 28
  31.1 196.8 %collective-permute-start.8 = (f32[2,1,192]{2,1,0:T(1,128)}, f32[2,1,192]{2,1,0:T(1,128)}, u32[]{:S(2)}, u32[]{:S(2)}) collective-permute-start(f32[2,1,192]{2,1,0:T(1,128)} %copy.68), channel_id=1, source_target_pairs={{1,0},{2,1},{3,2},{4,3},{5,4},{6,5},{7,6},{8,7},{9,8},{10,9},{11,1... | collective-permute-start | bytes 4616 | tf_op jit(solution)/shard_map/ppermute | solution.py:26
  40.2 1.9 copy-start.9
  96.3 5.4 %copy-start.2 = (f32[2,6,1536]{2,1,0:T(8,128)S(1)}, f32[2,6,1536]{2,1,0:T(8,128)}, u32[]{:S(2)}) copy-start(f32[2,6,1536]{2,1,0:T(8,128)} %copy.64) | copy-start | bytes 221188
  103.3 11.1 %copy-start.14 = (f32[2]{0:T(128)S(1)}, f32[2]{0:T(128)}, u32[]{:S(2)}) copy-start(f32[2]{0:T(128)} %multiply_reduce_fusion) | copy-start | bytes 28
  103.4 5.1 %collective-permute-start.2 = (f32[2,2,8,1,1536]{4,2,3,1,0:T(8,128)S(1)}, f32[2,2,8,1,1536]{4,2,3,1,0:T(8,128)S(1)}, u32[]{:S(2)}, u32[]{:S(2)}) collective-permute-start(f32[2,2,8,1,1536]{4,2,3,1,0:T(8,128)S(1)} %get-tuple-element.112), channel_id=1, source_target_pairs={{1,0},{2,1},{3,2},{4,3},{5,4},{6,5},{7,6},{8,7},{9,8},{10,9},{11,1... | collective-permute-start | bytes 589832 | tf_op jit(solution)/shard_map/ppermute | solution.py:26
  105.3 9.1 %collective-permute-start.3 = (f32[2,2,8,1,1536]{4,2,3,1,0:T(8,128)S(1)}, f32[2,2,8,1,1536]{4,2,3,1,0:T(8,128)S(1)}, u32[]{:S(2)}, u32[]{:S(2)}) collective-permute-start(f32[2,2,8,1,1536]{4,2,3,1,0:T(8,128)S(1)} %get-tuple-element.113), channel_id=1, source_target_pairs={{0,1},{1,2},{2,3},{3,4},{4,5},{5,6},{6,7},{7,8},{8,9},{9,10},{10,1... | collective-permute-start | bytes 589832 | tf_op jit(solution)/shard_map/ppermute | solution.py:23
  114.4 2.6 copy-start.3
  118.7 5.2 %copy-start.11 = (f32[2,1,192]{2,1,0:T(1,128)S(1)}, f32[2,1,192]{2,1,0:T(1,128)}, u32[]{:S(2)}) copy-start(f32[2,1,192]{2,1,0:T(1,128)} %copy.70) | copy-start | bytes 4612
  118.7 11.1 %copy-start.15 = (f32[2]{0:T(128)S(1)}, f32[2]{0:T(128)}, u32[]{:S(2)}) copy-start(f32[2]{0:T(128)} %multiply_reduce_fusion) | copy-start | bytes 28
  118.8 5.1 %collective-permute-start.4 = (f32[2,2,8,1,1536]{4,2,3,1,0:T(8,128)S(1)}, f32[2,2,8,1,1536]{4,2,3,1,0:T(8,128)S(1)}, u32[]{:S(2)}, u32[]{:S(2)}) collective-permute-start(f32[2,2,8,1,1536]{4,2,3,1,0:T(8,128)S(1)} %get-tuple-element.106), channel_id=1, source_target_pairs={{1,0},{2,1},{3,2},{4,3},{5,4},{6,5},{7,6},{8,7},{9,8},{10,9},{11,1... | collective-permute-start | bytes 589832 | tf_op jit(solution)/shard_map/ppermute | solution.py:26
  120.7 9.1 %collective-permute-start.5 = (f32[2,2,8,1,1536]{4,2,3,1,0:T(8,128)S(1)}, f32[2,2,8,1,1536]{4,2,3,1,0:T(8,128)S(1)}, u32[]{:S(2)}, u32[]{:S(2)}) collective-permute-start(f32[2,2,8,1,1536]{4,2,3,1,0:T(8,128)S(1)} %get-tuple-element.107), channel_id=1, source_target_pairs={{0,1},{1,2},{2,3},{3,4},{4,5},{5,6},{6,7},{7,8},{8,9},{9,10},{10,1... | collective-permute-start | bytes 589832 | tf_op jit(solution)/shard_map/ppermute | solution.py:23
  123.9 104.1 %collective-permute-start.9 = (f32[2,1,192]{2,1,0:T(1,128)S(1)}, f32[2,1,192]{2,1,0:T(1,128)S(1)}, u32[]{:S(2)}, u32[]{:S(2)}) collective-permute-start(f32[2,1,192]{2,1,0:T(1,128)S(1)} %copy-done.11), channel_id=1, source_target_pairs={{0,1},{1,2},{2,3},{3,4},{4,5},{5,6},{6,7},{7,8},{8,9},{9,10},{10,1... | collective-permute-start | bytes 4616 | tf_op jit(solution)/shard_map/ppermute | solution.py:23
  129.8 2.6 copy-start.4
  140.1 87.9 %copy-start.7 = (f32[2,6,192]{2,1,0:T(8,128)S(1)}, f32[2,6,192]{2,1,0:T(8,128)}, u32[]{:S(2)}) copy-start(f32[2,6,192]{2,1,0:T(8,128)} %copy-done.6) | copy-start | bytes 27652
  140.1 87.9 %copy-start.8 = (f32[6,192]{1,0:T(8,128)S(1)}, f32[6,192]{1,0:T(8,128)}, u32[]{:S(2)}) copy-start(f32[6,192]{1,0:T(8,128)} %param.21) | copy-start | bytes 13828
  140.1 299.0 %reduce-scatter.9.cloned.1.call-start = ((), (), s32[]{:S(2)}) async-start(), calls=%async_computation.3 | async-start | bytes 884736
  140.9 172.3 %collective-permute-start.6 = (f32[2,2,8,1,1536]{4,2,3,1,0:T(8,128)}, f32[2,2,8,1,1536]{4,2,3,1,0:T(8,128)}, u32[]{:S(2)}, u32[]{:S(2)}) collective-permute-start(f32[2,2,8,1,1536]{4,2,3,1,0:T(8,128)} %get-tuple-element.100), channel_id=1, source_target_pairs={{1,0},{2,1},{3,2},{4,3},{5,4},{6,5},{7,6},{8,7},{9,8},{10,9},{11,1... | collective-permute-start | bytes 589832 | tf_op jit(solution)/shard_map/ppermute | solution.py:26
  226.0 87.2 %collective-permute-start.7 = (f32[2,2,8,1,1536]{4,2,3,1,0:T(8,128)}, f32[2,2,8,1,1536]{4,2,3,1,0:T(8,128)}, u32[]{:S(2)}, u32[]{:S(2)}) collective-permute-start(f32[2,2,8,1,1536]{4,2,3,1,0:T(8,128)} %get-tuple-element.101), channel_id=1, source_target_pairs={{0,1},{1,2},{2,3},{3,4},{4,5},{5,6},{6,7},{7,8},{8,9},{9,10},{10,1... | collective-permute-start | bytes 589832 | tf_op jit(solution)/shard_map/ppermute | solution.py:23
  228.8 27.7 %collective-permute-start.12 = (f32[2,1,192]{2,1,0:T(1,128)S(1)}, f32[2,1,192]{2,1,0:T(1,128)S(1)}, u32[]{:S(2)}, u32[]{:S(2)}) collective-permute-start(f32[2,1,192]{2,1,0:T(1,128)S(1)} %get-tuple-element.128), channel_id=1, source_target_pairs={{1,0},{2,1},{3,2},{4,3},{5,4},{6,5},{7,6},{8,7},{9,8},{10,9},{11,1... | collective-permute-start | bytes 4616 | tf_op jit(solution)/shard_map/ppermute | solution.py:26
  234.6 21.9 %collective-permute-start.13 = (f32[2,1,192]{2,1,0:T(1,128)S(1)}, f32[2,1,192]{2,1,0:T(1,128)S(1)}, u32[]{:S(2)}, u32[]{:S(2)}) collective-permute-start(f32[2,1,192]{2,1,0:T(1,128)S(1)} %get-tuple-element.129), channel_id=1, source_target_pairs={{0,1},{1,2},{2,3},{3,4},{4,5},{5,6},{6,7},{7,8},{8,9},{9,10},{10,1... | collective-permute-start | bytes 4616 | tf_op jit(solution)/shard_map/ppermute | solution.py:23
  236.6 7.9 %collective-permute-start.14 = (f32[2,6,1]{2,1,0:T(8,128)S(1)}, f32[2,6,1]{2,1,0:T(8,128)S(1)}, u32[]{:S(2)}, u32[]{:S(2)}) collective-permute-start(f32[2,6,1]{2,1,0:T(8,128)S(1)} %get-tuple-element.130), channel_id=1, source_target_pairs={{64,0},{128,64},{192,128},{256,192},{320,256},{384,320},{448,384},... | collective-permute-start | bytes 152 | tf_op jit(solution)/shard_map/ppermute | solution.py:26
  244.5 12.0 %collective-permute-start.15 = (f32[2,6,1]{2,1,0:T(8,128)S(1)}, f32[2,6,1]{2,1,0:T(8,128)S(1)}, u32[]{:S(2)}, u32[]{:S(2)}) collective-permute-start(f32[2,6,1]{2,1,0:T(8,128)S(1)} %get-tuple-element.131), channel_id=1, source_target_pairs={{0,64},{64,128},{128,192},{192,256},{256,320},{320,384},{384,448},... | collective-permute-start | bytes 152 | tf_op jit(solution)/shard_map/ppermute | solution.py:23
  308.1 5.1 %copy-start.5 = (f32[2,8,6,1536]{3,1,2,0:T(8,128)S(1)}, f32[2,8,6,1536]{3,1,2,0:T(8,128)}, u32[]{:S(2)}) copy-start(f32[2,8,6,1536]{3,1,2,0:T(8,128)} %fusion.98) | copy-start | bytes 1769476
  308.1 5.1 %copy-start.16 = (f32[2]{0:T(128)S(1)}, f32[2]{0:T(128)}, u32[]{:S(2)}) copy-start(f32[2]{0:T(128)} %multiply_reduce_fusion) | copy-start | bytes 28
  308.8 131.5 %collective-permute-start.20 = (f32[2,1,192]{2,1,0:T(1,128)S(1)}, f32[2,1,192]{2,1,0:T(1,128)S(1)}, u32[]{:S(2)}, u32[]{:S(2)}) collective-permute-start(f32[2,1,192]{2,1,0:T(1,128)S(1)} %get-tuple-element.124), channel_id=1, source_target_pairs={{1,0},{2,1},{3,2},{4,3},{5,4},{6,5},{7,6},{8,7},{9,8},{10,9},{11,1... | collective-permute-start | bytes 4616 | tf_op jit(solution)/shard_map/ppermute | solution.py:26
  310.8 129.6 %collective-permute-start.21 = (f32[2,1,192]{2,1,0:T(1,128)S(1)}, f32[2,1,192]{2,1,0:T(1,128)S(1)}, u32[]{:S(2)}, u32[]{:S(2)}) collective-permute-start(f32[2,1,192]{2,1,0:T(1,128)S(1)} %get-tuple-element.125), channel_id=1, source_target_pairs={{0,1},{1,2},{2,3},{3,4},{4,5},{5,6},{6,7},{7,8},{8,9},{9,10},{10,1... | collective-permute-start | bytes 4616 | tf_op jit(solution)/shard_map/ppermute | solution.py:23
  320.1 8.4 %collective-permute-start.16 = (f32[2,2,8,1,1536]{4,2,3,1,0:T(8,128)S(1)}, f32[2,2,8,1,1536]{4,2,3,1,0:T(8,128)S(1)}, u32[]{:S(2)}, u32[]{:S(2)}) collective-permute-start(f32[2,2,8,1,1536]{4,2,3,1,0:T(8,128)S(1)} %get-tuple-element.92), channel_id=1, source_target_pairs={{1,0},{2,1},{3,2},{4,3},{5,4},{6,5},{7,6},{8,7},{9,8},{10,9},{11,1... | collective-permute-start | bytes 589832 | tf_op jit(solution)/shard_map/ppermute | solution.py:26
  325.4 9.1 %collective-permute-start.17 = (f32[2,2,8,1,1536]{4,2,3,1,0:T(8,128)S(1)}, f32[2,2,8,1,1536]{4,2,3,1,0:T(8,128)S(1)}, u32[]{:S(2)}, u32[]{:S(2)}) collective-permute-start(f32[2,2,8,1,1536]{4,2,3,1,0:T(8,128)S(1)} %get-tuple-element.93), channel_id=1, source_target_pairs={{0,1},{1,2},{2,3},{3,4},{4,5},{5,6},{6,7},{7,8},{8,9},{9,10},{10,1... | collective-permute-start | bytes 589832 | tf_op jit(solution)/shard_map/ppermute | solution.py:23
  338.8 5.1 %collective-permute-start.18 = (f32[2,2,8,1,1536]{4,2,3,1,0:T(8,128)S(1)}, f32[2,2,8,1,1536]{4,2,3,1,0:T(8,128)S(1)}, u32[]{:S(2)}, u32[]{:S(2)}) collective-permute-start(f32[2,2,8,1,1536]{4,2,3,1,0:T(8,128)S(1)} %get-tuple-element.86), channel_id=1, source_target_pairs={{1,0},{2,1},{3,2},{4,3},{5,4},{6,5},{7,6},{8,7},{9,8},{10,9},{11,1... | collective-permute-start | bytes 589832 | tf_op jit(solution)/shard_map/ppermute | solution.py:26
  340.7 9.1 %collective-permute-start.19 = (f32[2,2,8,1,1536]{4,2,3,1,0:T(8,128)S(1)}, f32[2,2,8,1,1536]{4,2,3,1,0:T(8,128)S(1)}, u32[]{:S(2)}, u32[]{:S(2)}) collective-permute-start(f32[2,2,8,1,1536]{4,2,3,1,0:T(8,128)S(1)} %get-tuple-element.87), channel_id=1, source_target_pairs={{0,1},{1,2},{2,3},{3,4},{4,5},{5,6},{6,7},{7,8},{8,9},{9,10},{10,1... | collective-permute-start | bytes 589832 | tf_op jit(solution)/shard_map/ppermute | solution.py:23
  355.9 84.4 %collective-permute-start.22 = (f32[2,6,1]{2,1,0:T(8,128)S(1)}, f32[2,6,1]{2,1,0:T(8,128)S(1)}, u32[]{:S(2)}, u32[]{:S(2)}) collective-permute-start(f32[2,6,1]{2,1,0:T(8,128)S(1)} %get-tuple-element.126), channel_id=1, source_target_pairs={{64,0},{128,64},{192,128},{256,192},{320,256},{384,320},{448,384},... | collective-permute-start | bytes 152 | tf_op jit(solution)/shard_map/ppermute | solution.py:26
  357.8 82.5 %collective-permute-start.23 = (f32[2,6,1]{2,1,0:T(8,128)S(1)}, f32[2,6,1]{2,1,0:T(8,128)S(1)}, u32[]{:S(2)}, u32[]{:S(2)}) collective-permute-start(f32[2,6,1]{2,1,0:T(8,128)S(1)} %get-tuple-element.127), channel_id=1, source_target_pairs={{0,64},{64,128},{128,192},{192,256},{256,320},{320,384},{384,448},... | collective-permute-start | bytes 152 | tf_op jit(solution)/shard_map/ppermute | solution.py:23
  362.6 103.6 %copy-start.10 = (f32[2,2,8,6,1536]{4,2,3,1,0:T(8,128)}, f32[2,2,8,6,1536]{4,2,3,1,0:T(8,128)S(1)}, u32[]{:S(2)}) copy-start(f32[2,2,8,6,1536]{4,2,3,1,0:T(8,128)S(1)} %scatter.29) | copy-start | bytes 3538948
  440.4 25.0 %collective-permute-start.24 = (f32[2,1,192]{2,1,0:T(1,128)S(1)}, f32[2,1,192]{2,1,0:T(1,128)S(1)}, u32[]{:S(2)}, u32[]{:S(2)}) collective-permute-start(f32[2,1,192]{2,1,0:T(1,128)S(1)} %get-tuple-element.120), channel_id=1, source_target_pairs={{1,0},{2,1},{3,2},{4,3},{5,4},{6,5},{7,6},{8,7},{9,8},{10,9},{11,1... | collective-permute-start | bytes 4616 | tf_op jit(solution)/shard_map/ppermute | solution.py:26
  443.9 21.6 %collective-permute-start.25 = (f32[2,1,192]{2,1,0:T(1,128)S(1)}, f32[2,1,192]{2,1,0:T(1,128)S(1)}, u32[]{:S(2)}, u32[]{:S(2)}) collective-permute-start(f32[2,1,192]{2,1,0:T(1,128)S(1)} %get-tuple-element.121), channel_id=1, source_target_pairs={{0,1},{1,2},{2,3},{3,4},{4,5},{5,6},{6,7},{7,8},{8,9},{9,10},{10,1... | collective-permute-start | bytes 4616 | tf_op jit(solution)/shard_map/ppermute | solution.py:23
  445.9 9.9 %collective-permute-start.26 = (f32[2,6,1]{2,1,0:T(8,128)S(1)}, f32[2,6,1]{2,1,0:T(8,128)S(1)}, u32[]{:S(2)}, u32[]{:S(2)}) collective-permute-start(f32[2,6,1]{2,1,0:T(8,128)S(1)} %get-tuple-element.122), channel_id=1, source_target_pairs={{64,0},{128,64},{192,128},{256,192},{320,256},{384,320},{448,384},... | collective-permute-start | bytes 152 | tf_op jit(solution)/shard_map/ppermute | solution.py:26
  453.9 11.6 %collective-permute-start.27 = (f32[2,6,1]{2,1,0:T(8,128)S(1)}, f32[2,6,1]{2,1,0:T(8,128)S(1)}, u32[]{:S(2)}, u32[]{:S(2)}) collective-permute-start(f32[2,6,1]{2,1,0:T(8,128)S(1)} %get-tuple-element.123), channel_id=1, source_target_pairs={{0,64},{64,128},{128,192},{192,256},{256,320},{320,384},{384,448},... | collective-permute-start | bytes 152 | tf_op jit(solution)/shard_map/ppermute | solution.py:23
Sparse Core Ops, SparseCore 0:
  140.2 84.5 reduce-scatter.6
  355.9 83.1 reduce-scatter.8
where the time goes:
time: 474 us; the launch traced here: 473 us
  waiting for transfers between devices  204 us (43%)
  blocking collectives  102 us (22%)
  starting transfers between devices  93.5 us (20%)
  local copies, waits for them, and re-layouts  29.9 us (6%)
  matrix products  21.1 us (4%)
  between operations  14.8 us (3%)
  other arithmetic  7.27 us (2%)
    unnamed x4, waiting for transfers between devices  159 us
    all_gather x2, blocking collectives, body(): surface = lax.all_gather(ocean, 'member', axis=2, tiled=True)  102 us
    ppermute x14, starting transfers between devices, with_halo(): lax.ppermute(lax.slice_in_dim(block, 0, width, axis=dim), axis, backward)  62.5 us
    ppermute x14, waiting for transfers between devices, with_halo(): lax.ppermute(lax.slice_in_dim(block, block.shape[dim] - width, None, axis...  41.4 us
    ppermute x14, starting transfers between devices, with_halo(): lax.ppermute(lax.slice_in_dim(block, block.shape[dim] - width, None, axis...  31 us
    dot_general x6, matrix products, atmos_step(): jnp.einsum('kl,fmlrn->fmkrn', level_mix, advected, precision=lax.Precisio...  20.9 us
  transfers between devices with their start and end apart: 30, of which 13 were waited for; matrix products, arithmetic and copies ran while one was open for 12% of the time, Pallas kernels for 0%

commit v1 on v0

v1 whole, which is shorter than its diff:
```python
import functools

import jax
import jax.numpy as jnp
from jax import lax
from jax.experimental import pallas as pl
from jax.experimental.pallas import tpu as pltpu
from jax.sharding import PartitionSpec as P

ADVECTION = 0.1
OCEAN_GAIN = 0.5
OCEAN_DIFFUSION = 0.15
MESH = pl.DeviceIdType.MESH
F32 = jnp.float32
LANES = 128
CHUNK = 512


def tiles(vector, count):
    return jnp.concatenate([vector] * count, axis=1)


def sublane(shape):
    return lax.broadcasted_iota(jnp.int32, shape, 0)


def stack_rows(south, own, north):
    index = sublane(own.shape)
    middle = pltpu.roll(own, 4, 0)
    low = jnp.where(index < 4, pltpu.roll(south, 6, 0), middle)
    high = jnp.where(index < 2, middle, pltpu.roll(north, 2, 0))
    return jnp.concatenate([low, high], axis=0)


def join_chunks(even, odd):
    lane = lax.broadcasted_iota(jnp.int32, (8, LANES), 1)
    first = pltpu.roll(odd[:, :LANES], 64, 1)
    second = pltpu.roll(odd[:, LANES:], 64, 1)
    return jnp.concatenate(
        [even[:, :LANES], jnp.where(lane < 64, even[:, LANES:], first), jnp.where(lane < 64, first, second)], axis=1
    )


def kernel(
    nx, nlat, scale,
    atm, ocean_in, visc_in, mask_in, pick, table, mixing, atm_out, ocean_out,
    state, coef, diff, surf, chunks, masks, ocean, visc, mask, force, part, gather_x, total, gather_y, gather_f, seg,
    load_sem, halo_send, halo_recv, seg_send, seg_recv, pair_send, pair_recv, mask_send, mask_recv,
    x_send, x_recv, y_send, y_recv, f_send, f_recv, out_sem,
):
    me = lax.axis_index("member")
    lat = lax.axis_index("lat")
    x, yh = lax.rem(me, nx), lax.div(me, nx)
    has_south, has_north = lat > 0, lat < nlat - 1
    partner = ((1 - yh) * nx + x, lat)
    lon = mask_in.shape[1]
    pieces = lon // CHUNK
    quarter = lon // nx

    def peers():
        for side in (-1, 0, 1):
            for step in range(nx):
                if side or step:
                    yield side, step, (yh * nx + lax.rem(x + step, nx), lat + side)

    def guarded(side, run):
        if side < 0:
            pl.when(has_south)(run)
        elif side > 0:
            pl.when(has_north)(run)
        else:
            run()

    loads = [pltpu.make_async_copy(atm.at[:, :, r], state.at[0, r + 3], load_sem.at[r]) for r in range(6)]
    for load in loads:
        load.start()

    barrier = pltpu.get_barrier_semaphore()
    pl.semaphore_signal(barrier, inc=1, device_id=partner, device_id_type=MESH)
    for side, step, device in peers():
        guarded(side, lambda device=device: pl.semaphore_signal(barrier, inc=1, device_id=device, device_id_type=MESH))

    lane_pad = jnp.zeros((8, 2 * LANES), F32)
    for field in range(3):
        seg[field] = lane_pad
        for r in range(6):
            line = visc_in[r : r + 1, :] if field == 2 else ocean_in[r, field : field + 1, :]
            seg[field, r : r + 1, 0:192] = line
    masks[1] = jnp.zeros((8, lon), F32)
    masks[1, 0:6, :] = mask_in[...].astype(F32)
    row_zero = jnp.zeros((2, 2, 8, lon), F32)

    @pl.when(lat == 0)
    def _():
        for b in range(6):
            state[b, 2] = row_zero
        masks[0] = jnp.zeros((8, lon), F32)
        for a in range(2):
            for i in range(nx):
                chunks[a, 0, i] = jnp.zeros((3, 8, 2 * LANES), F32)
                gather_f[a, 0, i] = jnp.zeros((2, 8, quarter), F32)

    @pl.when(lat == nlat - 1)
    def _():
        for b in range(6):
            state[b, 9] = row_zero
        masks[2] = jnp.zeros((8, lon), F32)
        for a in range(2):
            for i in range(nx):
                chunks[a, 2, i] = jnp.zeros((3, 8, 2 * LANES), F32)
                gather_f[a, 2, i] = jnp.zeros((2, 8, quarter), F32)

    pl.semaphore_wait(barrier, nx + nx * has_south.astype(jnp.int32) + nx * has_north.astype(jnp.int32))

    def halo(cp, side, depth):
        row = 5 - depth if side > 0 else depth
        there = 2 - depth if side > 0 else 9 + depth
        source = atm.at[:, :, row] if cp == 0 else state.at[3, row + 3]
        k = (side + 1) // 2
        return pltpu.make_async_remote_copy(
            source, state.at[3 * cp, there], halo_send.at[cp, k, depth], halo_recv.at[cp, k, depth],
            device_id=(me, lat + side), device_id_type=MESH,
        )

    def start_halos(cp):
        for depth in range(3):
            for side in (-1, 1):
                guarded(side, lambda side=side, depth=depth: halo(cp, side, depth).start())

    def wait_halo(cp, depth):
        for side in (-1, 1):
            guarded(-side, lambda side=side: halo(cp, side, depth).wait_recv())

    def spread(stage, side, step, device):
        source = seg if stage == 0 else chunks.at[1 - yh, 1, x]
        target = chunks.at[yh if stage == 0 else 1 - yh, 1 - side, x]
        return pltpu.make_async_remote_copy(
            source, target, seg_send.at[stage, side + 1, step], seg_recv.at[stage, side + 1, step],
            device_id=device, device_id_type=MESH,
        )

    pair = pltpu.make_async_remote_copy(
        seg, chunks.at[yh, 1, x], pair_send, pair_recv, device_id=partner, device_id_type=MESH
    )

    def send_mask(side):
        return pltpu.make_async_remote_copy(
            masks.at[1], masks.at[1 - side], mask_send.at[(side + 1) // 2], mask_recv.at[(side + 1) // 2],
            device_id=(me, lat + side), device_id_type=MESH,
        )

    pair.start()
    start_halos(0)
    for side, step, device in peers():
        guarded(side, lambda a=(side, step, device): spread(0, *a).start())
    for side in (-1, 1):
        guarded(side, lambda side=side: send_mask(side).start())
    chunks[yh, 1, x] = seg[...]

    sub = sublane((8, LANES))
    top = sub == 0
    dif = [0.6 * table[0, pick[m]] for m in range(2)]
    exc = [[2.0 * table[1 + c, pick[m]] for m in range(2)] for c in range(2)]
    exv = [[jnp.where(top, exc[c][m], 0.0) for m in range(2)] for c in range(2)]
    mix = mixing[...]
    row8 = lax.broadcasted_iota(jnp.int32, (8, 8), 0)
    col8 = lax.broadcasted_iota(jnp.int32, (8, 8), 1)
    for m in range(2):
        diff[m, 0] = jnp.full((8, LANES), dif[m], F32)
        diff[m, 1] = jnp.full((8, LANES), 1.0 - 4.0 * dif[m], F32)
    for r in range(8):
        diagonal = jnp.sum(jnp.where(col8 == lax.rem(row8 - r + 8, 8), mix, 0.0), axis=1, keepdims=True)
        value = jnp.broadcast_to(diagonal, (8, LANES))
        if r == 0:
            value = value + 1.0
        for c in range(2):
            for m in range(2):
                coef[c, m, r] = jnp.where(top, value * (1.0 - exc[c][m]), value)

    def unit(source, target, row, m, k, with_surface):
        e = row + 3
        width = CHUNK // LANES
        off = pl.multiple_of(k * CHUNK, CHUNK)
        right = pl.multiple_of(lax.rem(k + 1, pieces) * CHUNK, LANES)
        left = pl.multiple_of(lax.rem(k * CHUNK + lon - LANES, lon), LANES)
        d = tiles(diff[m, 0], width)
        d4 = tiles(diff[m, 1], width)
        wind = None
        for c in (1, 0):
            centre = state[source, e, c, m, :, pl.ds(off, CHUNK)]
            ahead = state[source, e, c, m, :, pl.ds(right, LANES)]
            behind = state[source, e, c, m, :, pl.ds(left, LANES)]
            north = state[source, e + 1, c, m, :, pl.ds(off, CHUNK)]
            south = state[source, e - 1, c, m, :, pl.ds(off, CHUNK)]
            east = pltpu.roll(jnp.concatenate([centre, ahead], axis=1), CHUNK + LANES - 1, 1)[:, :CHUNK]
            west = pltpu.roll(jnp.concatenate([centre, behind], axis=1), 1, 1)[:, :CHUNK]
            if c == 1:
                wind = (ADVECTION * 0.5) * centre
            advected = d4 * centre + d * ((east + west) + (north + south)) - wind * (east - west)
            value = tiles(coef[c, m, 0], width) * advected
            for r in range(1, 8):
                value = value + tiles(coef[c, m, r], width) * pltpu.roll(advected, r, 0)
            if with_surface:
                value = value + surf[row + 2, c, m, :, pl.ds(off, CHUNK)]
            state[target, e, c, m, :, pl.ds(off, CHUNK)] = value

    def rows(source, target, first, stride, count, with_surface):
        each = 2 * pieces

        def body(t, carry):
            row = first + (t // each) * stride
            m = lax.rem(t // pieces, 2)
            k = lax.rem(t, pieces)
            inside = ((row >= 0) | has_south) & ((row <= 5) | has_north)

            @pl.when(inside)
            def _():
                unit(source, target, row, m, k, with_surface)

            return carry

        lax.fori_loop(0, count * each, body, 0)

    def add_surface(target):
        for row in range(-2, 8):
            for c in range(2):
                line = jnp.broadcast_to(ocean[c, row + 4 : row + 5, :], (8, lon))
                for m in range(2):
                    value = tiles(exv[c][m], lon // LANES) * line
                    surf[row + 2, c, m] = value

                    def run(value=value, c=c, m=m, row=row):
                        state[target, row + 3, c, m] = state[target, row + 3, c, m] + value

                    guarded(-1 if row < 0 else 1 if row > 5 else 0, run)

    def first_rows(cp, depth):
        wait_halo(cp, depth)
        low = -depth
        rows(3 * cp, 3 * cp + 1, low, 5 - 2 * low, 2, False)

    def ocean_steps(cp):
        for c in range(2):
            for q in range(nx):
                blocks = [gather_f[cp, side, q, c] for side in range(3)]
                force[c, :, q * quarter : (q + 1) * quarter] = stack_rows(*blocks)
        for _ in range(2):
            for c in range(2):
                here = ocean[c]
                lap = (
                    pltpu.roll(here, lon - 1, 1) + pltpu.roll(here, 1, 1)
                    + pltpu.roll(here, 15, 0) + pltpu.roll(here, 1, 0) - 4.0 * here
                )
                rate = visc[...] if c == 1 else OCEAN_DIFFUSION
                ocean[c] = here + mask[...] * (OCEAN_GAIN * force[c] + rate * lap)

    def send_x(cp, step):
        to = lax.rem(x + step, nx)
        return pltpu.make_async_remote_copy(
            part.at[cp, to], gather_x.at[cp, step - 1], x_send.at[cp, step - 1], x_recv.at[cp, step - 1],
            device_id=(yh * nx + to, lat), device_id_type=MESH,
        )

    def send_y(cp):
        return pltpu.make_async_remote_copy(
            total.at[cp], gather_y.at[cp], y_send.at[cp], y_recv.at[cp], device_id=partner, device_id_type=MESH
        )

    def send_f(cp, side, step, device):
        return pltpu.make_async_remote_copy(
            gather_f.at[cp, 1, x], gather_f.at[cp, 1 - side, x], f_send.at[cp, side + 1, step],
            f_recv.at[cp, side + 1, step], device_id=device, device_id_type=MESH,
        )

    def flux(cp):
        last = 3 * cp + 3
        count = lon // LANES
        for c in range(2):
            weights = [tiles(exv[c][m], count) for m in range(2)]
            own = pltpu.roll(ocean[c], 12, 0)[0:8]
            value = jnp.zeros((8, lon), F32)
            for row in range(6):
                line = weights[0] * state[last, row + 3, c, 0] + weights[1] * state[last, row + 3, c, 1]
                value = value + (pltpu.roll(line, row, 0) if row else line)
            value = value - (exc[c][0] + exc[c][1]) * own
            for q in range(nx):
                part[cp, q, c] = value[:, q * quarter : (q + 1) * quarter]

    def stage_y(cp):
        for step in range(1, nx):
            send_x(cp, step).wait_recv()
        total[cp] = (part[cp, x] + gather_x[cp, 0]) + (gather_x[cp, 1] + gather_x[cp, 2])
        send_y(cp).start()

    def stage_f(cp):
        send_y(cp).wait_recv()
        gather_f[cp, 1, x] = (total[cp] + gather_y[cp]) * scale
        for side, step, device in peers():
            guarded(side, lambda a=(side, step, device): send_f(cp, *a).start())

    def wait_f(cp):
        for side, step, device in peers():
            guarded(-side, lambda a=(side, step, device): send_f(cp, *a).wait_recv())

    for load in loads:
        load.wait()
    rows(0, 1, 1, 1, 4, False)
    pair.wait_recv()
    for side, step, device in peers():
        guarded(side, lambda a=(side, step, device): spread(1, *a).start())
    for depth in range(3):
        first_rows(0, depth)
    for stage in range(2):
        for side, step, device in peers():
            guarded(-side, lambda a=(stage, side, step, device): spread(*a).wait_recv())
    for field in range(3):
        for q in range(nx):
            blocks = []
            for side in range(3):
                even = chunks[(2 * q) // nx, side, (2 * q) % nx, field]
                odd = chunks[(2 * q + 1) // nx, side, (2 * q + 1) % nx, field]
                blocks.append(join_chunks(even, odd))
            value = stack_rows(*blocks)
            columns = slice(q * quarter, (q + 1) * quarter)
            if field == 2:
                visc[:, columns] = value
            else:
                ocean[field, :, columns] = value
    add_surface(1)
    rows(1, 2, -1, 1, 8, True)
    rows(2, 3, 0, 1, 6, True)
    flux(0)
    for step in range(1, nx):
        send_x(0, step).start()
    start_halos(1)
    rows(3, 4, 1, 1, 4, False)
    stage_y(0)
    first_rows(1, 0)
    first_rows(1, 1)
    stage_f(0)
    first_rows(1, 2)
    for side in (-1, 1):
        guarded(-side, lambda side=side: send_mask(side).wait_recv())
    mask[...] = stack_rows(masks[0], masks[1], masks[2])
    wait_f(0)
    ocean_steps(0)

    add_surface(4)
    rows(4, 5, -1, 1, 8, True)
    rows(5, 6, 0, 1, 6, True)
    flux(1)
    for step in range(1, nx):
        send_x(1, step).start()
    stores = [pltpu.make_async_copy(state.at[6, r + 3], atm_out.at[:, :, r], out_sem.at[r]) for r in range(6)]
    for store in stores:
        store.start()
    stage_y(1)
    stage_f(1)
    wait_f(1)
    ocean_steps(1)
    start = pl.multiple_of(((3 * me) // 2) * LANES, LANES)
    odd = lax.rem(me, 2) == 1
    for c in range(2):
        value = ocean[c, :, pl.ds(start, 2 * LANES)]
        value = jnp.where(odd, pltpu.roll(value, 192, 1), value)
        for r in range(6):
            ocean_out[r, c : c + 1, :] = value[r + 4 : r + 5, 0:192]

    for store in stores:
        store.wait()
    pair.wait_send()
    for side in (-1, 1):
        guarded(side, lambda side=side: send_mask(side).wait_send())
        for cp in range(2):
            for depth in range(3):
                guarded(side, lambda a=(cp, side, depth): halo(*a).wait_send())
    for stage in range(2):
        for side, step, device in peers():
            guarded(side, lambda a=(stage, side, step, device): spread(*a).wait_send())
    for cp in range(2):
        send_y(cp).wait_send()
        for step in range(1, nx):
            send_x(cp, step).wait_send()
        for side, step, device in peers():
            guarded(side, lambda a=(cp, side, step, device): send_f(*a).wait_send())


def body(nx, nlat, atmosphere, ocean_state, viscosity, sea_mask, parameter_index, parameter_table, level_mix):
    lon = atmosphere.shape[4]
    quarter = lon // nx
    vmem = pl.BlockSpec(memory_space=pltpu.VMEM)
    smem = pl.BlockSpec(memory_space=pltpu.SMEM)
    hbm = pl.BlockSpec(memory_space=pl.ANY)
    dma = pltpu.SemaphoreType.DMA
    fields = jnp.transpose(atmosphere, (0, 1, 3, 2, 4))
    atm_out, ocean_out = pl.pallas_call(
        functools.partial(kernel, nx, nlat, 1.0 / (4 * nx)),
        out_shape=(
            jax.ShapeDtypeStruct(fields.shape, F32),
            jax.ShapeDtypeStruct((6, 2, 192), F32),
        ),
        in_specs=[hbm, vmem, vmem, vmem, smem, smem, vmem],
        out_specs=(hbm, vmem),
        scratch_shapes=[
            pltpu.VMEM((7, 12, 2, 2, 8, lon), F32),
            pltpu.VMEM((2, 2, 8, 8, LANES), F32),
            pltpu.VMEM((2, 2, 8, LANES), F32),
            pltpu.VMEM((10, 2, 2, 8, lon), F32),
            pltpu.VMEM((2, 3, nx, 3, 8, 2 * LANES), F32),
            pltpu.VMEM((3, 8, lon), F32),
            pltpu.VMEM((2, 16, lon), F32),
            pltpu.VMEM((16, lon), F32),
            pltpu.VMEM((16, lon), F32),
            pltpu.VMEM((2, 16, lon), F32),
            pltpu.VMEM((2, nx, 2, 8, quarter), F32),
            pltpu.VMEM((2, nx - 1, 2, 8, quarter), F32),
            pltpu.VMEM((2, 2, 8, quarter), F32),
            pltpu.VMEM((2, 2, 8, quarter), F32),
            pltpu.VMEM((2, 3, nx, 2, 8, quarter), F32),
            pltpu.VMEM((3, 8, 2 * LANES), F32),
            dma((6,)),
            dma((2, 2, 3)),
            dma((2, 2, 3)),
            dma((2, 3, nx)),
            dma((2, 3, nx)),
            dma(()),
            dma(()),
            dma((2,)),
            dma((2,)),
            dma((2, nx - 1)),
            dma((2, nx - 1)),
            dma((2,)),
            dma((2,)),
            dma((2, 3, nx)),
            dma((2, 3, nx)),
            dma((6,)),
        ],
        compiler_params=pltpu.CompilerParams(
            collective_id=0, has_side_effects=True, vmem_limit_bytes=48 * 1024 * 1024
        ),
        name="coupled_window",
    )(
        fields,
        jnp.transpose(ocean_state, (1, 0, 2)),
        viscosity,
        sea_mask,
        parameter_index,
        jnp.transpose(parameter_table),
        level_mix,
    )
    return jnp.transpose(atm_out, (0, 1, 3, 2, 4)), jnp.transpose(ocean_out, (1, 0, 2))


def solution(mesh):
    return jax.shard_map(
        functools.partial(body, mesh.shape["member"] // 2, mesh.shape["lat"]),
        mesh=mesh,
        in_specs=(
            P(None, "member", None, "lat", None),
            P(None, "lat", "member"),
            P("lat", "member"),
            P("lat", None),
            P("member"),
            P(),
            P(),
        ),
        out_specs=(P(None, "member", None, "lat", None), P(None, "lat", "member")),
        check_vma=False,
    )
```

time: 474 us -> 105 us (0.22)
  the two profiles are of different devices: /device:TPU:48 before, /device:TPU:8 now
where the time goes in v1:
time: 105 us; the launch traced here: 104 us
  Pallas kernels  96 us (91%)
  local copies, waits for them, and re-layouts  7.1 us (7%)
    pallas_call x1, Pallas kernels, body(): pl.pallas_call(functools.partial(kernel, nx, nlat, 1.0 / (4 * nx)), out_s...  96 us
    unnamed x16, local copies, waits for them, and re-layouts  7.1 us

profile of v1, /device:TPU:8, one launch (start us, length us, event | category | flops | bytes accessed | tf_op | source)
XLA Modules:
  0.0 103.8 jit_solution(26810062559980602)
XLA Ops:
  0.6 0.0 copy-start
  0.6 1.3 %copy-done = f32[2,2,8,6,1536]{4,2,3,1,0:T(8,128)S(1)} copy-done((f32[2,2,8,6,1536]{4,2,3,1,0:T(8,128)S(1)}, f32[2,2,8,6,1536]{4,2,3,1,0:T(8,128)}, u32[]{:S(2)}) %copy-start) | copy-done | bytes 1179672
  1.9 0.0 copy-start.1
  1.9 0.8 copy-done.1
  2.7 0.0 copy-start.2
  2.7 0.7 copy-done.2
  3.4 0.0 copy-start.3
  3.4 0.7 copy-done.3
  4.1 0.0 copy-start.4
  4.1 0.7 copy-done.4
  4.8 0.0 copy-start.5
  4.8 0.7 copy-done.5
  5.5 0.0 copy-start.6
  5.5 0.7 copy-done.6
  6.1 96.0 %coupled_window.1 = (f32[2,2,6,8,1536]{4,3,2,1,0:T(8,128)S(1)}, f32[6,2,192]{2,1,0:T(2,128)S(1)}) custom-call(f32[2,2,6,8,1536]{4,3,2,1,0:T(8,128)S(1)} %bitcast.5, f32[6,2,192]{2,1,0:T(2,128)S(1)} %bitcast.7, f32[6,192]{1,0:T(8,128)S(1)} %copy-done.3, s32[6,1536]{1,0:T(8,128)S(1)} %copy-done.1, s32[2]{0:T(128)S(1)} %copy-done.6, f32[3,32]{1,0:T(4,128)S(1)} %bitcast.9, ...), custom_call_target="tpu_custom_call" | custom-call | tf_op jit(solution)/shard_map/coupled_window/pallas_call | solution.py:396
  102.1 1.0 copy.11
  103.2 0.6 copy.12
Async XLA Ops:
  0.6 1.3 %copy-start = (f32[2,2,8,6,1536]{4,2,3,1,0:T(8,128)S(1)}, f32[2,2,8,6,1536]{4,2,3,1,0:T(8,128)}, u32[]{:S(2)}) copy-start(f32[2,2,8,6,1536]{4,2,3,1,0:T(8,128)} %param.7) | copy-start | bytes 3538948
  1.9 0.8 copy-start.1
  2.7 0.7 copy-start.2
  3.4 0.7 copy-start.3
  4.1 0.7 copy-start.4
  4.8 0.7 copy-start.5
  5.5 0.7 copy-start.6

commit v2 on v1

--- a/solution.py
+++ b/solution.py
@@ -43,10 +43,11 @@
 
 def kernel(
     nx, nlat, scale,
-    atm, ocean_in, visc_in, mask_in, pick, table, mixing, atm_out, ocean_out,
+    atm, ocean_hbm, visc_hbm, mask_hbm, pick_hbm, table_hbm, mixing_hbm, atm_out, ocean_out,
+    ocean_in, visc_in, mask_in, pick, table, mixing,
     state, coef, diff, surf, chunks, masks, ocean, visc, mask, force, part, gather_x, total, gather_y, gather_f, seg,
     load_sem, halo_send, halo_recv, seg_send, seg_recv, pair_send, pair_recv, mask_send, mask_recv,
-    x_send, x_recv, y_send, y_recv, f_send, f_recv, out_sem,
+    x_send, x_recv, y_send, y_recv, f_send, f_recv, out_sem, small_sem,
 ):
     me = lax.axis_index("member")
     lat = lax.axis_index("lat")
@@ -72,6 +73,17 @@
             run()
 
     loads = [pltpu.make_async_copy(atm.at[:, :, r], state.at[0, r + 3], load_sem.at[r]) for r in range(6)]
+    small = [
+        pltpu.make_async_copy(source, target, small_sem.at[i])
+        for i, (source, target) in enumerate(
+            (
+                (ocean_hbm, ocean_in), (visc_hbm, visc_in), (mask_hbm, mask_in),
+                (pick_hbm, pick), (table_hbm, table), (mixing_hbm, mixing),
+            )
+        )
+    ]
+    for load in small:
+        load.start()
     for load in loads:
         load.start()
 
@@ -79,6 +91,9 @@
     pl.semaphore_signal(barrier, inc=1, device_id=partner, device_id_type=MESH)
     for side, step, device in peers():
         guarded(side, lambda device=device: pl.semaphore_signal(barrier, inc=1, device_id=device, device_id_type=MESH))
+
+    for load in small:
+        load.wait()
 
     lane_pad = jnp.zeros((8, 2 * LANES), F32)
     for field in range(3):
@@ -167,7 +182,8 @@
     col8 = lax.broadcasted_iota(jnp.int32, (8, 8), 1)
     for m in range(2):
         diff[m, 0] = jnp.full((8, LANES), dif[m], F32)
-        diff[m, 1] = jnp.full((8, LANES), 1.0 - 4.0 * dif[m], F32)
+        diff[m, 1] = jnp.full((8, LANES), 1.0 - 4.0 * dif[m], F32) / diff[m, 0]
+        diff[m, 0] = (0.5 * ADVECTION) / diff[m, 0]
     for r in range(8):
         diagonal = jnp.sum(jnp.where(col8 == lax.rem(row8 - r + 8, 8), mix, 0.0), axis=1, keepdims=True)
         value = jnp.broadcast_to(diagonal, (8, LANES))
@@ -175,51 +191,51 @@
             value = value + 1.0
         for c in range(2):
             for m in range(2):
-                coef[c, m, r] = jnp.where(top, value * (1.0 - exc[c][m]), value)
-
-    def unit(source, target, row, m, k, with_surface):
-        e = row + 3
+                weight = dif[m] * jnp.where(top, value * (1.0 - exc[c][m]), value)
+                coef[c, m, r] = pltpu.roll(weight, 4, 0) if r >= 4 else weight
+
+    def unit(source, target, e, m, k, with_surface):
         width = CHUNK // LANES
-        off = pl.multiple_of(k * CHUNK, CHUNK)
-        right = pl.multiple_of(lax.rem(k + 1, pieces) * CHUNK, LANES)
-        left = pl.multiple_of(lax.rem(k * CHUNK + lon - LANES, lon), LANES)
-        d = tiles(diff[m, 0], width)
-        d4 = tiles(diff[m, 1], width)
+        off, right, left = k * CHUNK, (k + 1) % pieces * CHUNK, (k * CHUNK - LANES) % lon
+        gain = tiles(diff[m, 0], width)
+        keep = tiles(diff[m, 1], width)
         wind = None
         for c in (1, 0):
-            centre = state[source, e, c, m, :, pl.ds(off, CHUNK)]
-            ahead = state[source, e, c, m, :, pl.ds(right, LANES)]
-            behind = state[source, e, c, m, :, pl.ds(left, LANES)]
-            north = state[source, e + 1, c, m, :, pl.ds(off, CHUNK)]
-            south = state[source, e - 1, c, m, :, pl.ds(off, CHUNK)]
+            centre = state[source, e, c, m, :, off : off + CHUNK]
+            ahead = state[source, e, c, m, :, right : right + LANES]
+            behind = state[source, e, c, m, :, left : left + LANES]
+            north = state[source, e + 1, c, m, :, off : off + CHUNK]
+            south = state[source, e - 1, c, m, :, off : off + CHUNK]
             east = pltpu.roll(jnp.concatenate([centre, ahead], axis=1), CHUNK + LANES - 1, 1)[:, :CHUNK]
             west = pltpu.roll(jnp.concatenate([centre, behind], axis=1), 1, 1)[:, :CHUNK]
             if c == 1:
-                wind = (ADVECTION * 0.5) * centre
-            advected = d4 * centre + d * ((east + west) + (north + south)) - wind * (east - west)
-            value = tiles(coef[c, m, 0], width) * advected
-            for r in range(1, 8):
-                value = value + tiles(coef[c, m, r], width) * pltpu.roll(advected, r, 0)
+                wind = gain * centre
+            advected = keep * centre + ((east + west) + (north + south)) - wind * (east - west)
+            near = tiles(coef[c, m, 0], width) * advected
+            far = tiles(coef[c, m, 4], width) * advected
+            for r in range(1, 4):
+                turned = pltpu.roll(advected, r, 0)
+                near = near + tiles(coef[c, m, r], width) * turned
+                far = far + tiles(coef[c, m, r + 4], width) * turned
+            value = near + pltpu.roll(far, 4, 0)
             if with_surface:
-                value = value + surf[row + 2, c, m, :, pl.ds(off, CHUNK)]
-            state[target, e, c, m, :, pl.ds(off, CHUNK)] = value
+                value = value + surf[e - 1, c, m, :, off : off + CHUNK]
+            state[target, e, c, m, :, off : off + CHUNK] = value
 
     def rows(source, target, first, stride, count, with_surface):
-        each = 2 * pieces
-
-        def body(t, carry):
-            row = first + (t // each) * stride
-            m = lax.rem(t // pieces, 2)
-            k = lax.rem(t, pieces)
+        def body(i, carry):
+            row = first + i * stride
             inside = ((row >= 0) | has_south) & ((row <= 5) | has_north)
 
             @pl.when(inside)
             def _():
-                unit(source, target, row, m, k, with_surface)
+                for m in range(2):
+                    for k in range(pieces):
+                        unit(source, target, row + 3, m, k, with_surface)
 
             return carry
 
-        lax.fori_loop(0, count * each, body, 0)
+        lax.fori_loop(0, count, body, 0)
 
     def add_surface(target):
         for row in range(-2, 8):
@@ -389,7 +405,6 @@
     lon = atmosphere.shape[4]
     quarter = lon // nx
     vmem = pl.BlockSpec(memory_space=pltpu.VMEM)
-    smem = pl.BlockSpec(memory_space=pltpu.SMEM)
     hbm = pl.BlockSpec(memory_space=pl.ANY)
     dma = pltpu.SemaphoreType.DMA
     fields = jnp.transpose(atmosphere, (0, 1, 3, 2, 4))
@@ -399,9 +414,15 @@
             jax.ShapeDtypeStruct(fields.shape, F32),
             jax.ShapeDtypeStruct((6, 2, 192), F32),
         ),
-        in_specs=[hbm, vmem, vmem, vmem, smem, smem, vmem],
+        in_specs=[hbm] * 7,
         out_specs=(hbm, vmem),
         scratch_shapes=[
+            pltpu.VMEM((6, 2, 192), F32),
+            pltpu.VMEM((6, 192), F32),
+            pltpu.VMEM((6, lon), jnp.int32),
+            pltpu.SMEM((2,), jnp.int32),
+            pltpu.SMEM(parameter_table.shape[::-1], F32),
+            pltpu.VMEM((8, 8), F32),
             pltpu.VMEM((7, 12, 2, 2, 8, lon), F32),
             pltpu.VMEM((2, 2, 8, 8, LANES), F32),
             pltpu.VMEM((2, 2, 8, LANES), F32),
@@ -434,9 +455,10 @@
             dma((2, 3, nx)),
             dma((2, 3, nx)),
             dma((6,)),
+            dma((6,)),
         ],
         compiler_params=pltpu.CompilerParams(
-            collective_id=0, has_side_effects=True, vmem_limit_bytes=48 * 1024 * 1024
+            collective_id=0, has_side_effects=True, vmem_limit_bytes=67043328
         ),
         name="coupled_window",
     )(

time: 105 us -> 71.9 us (0.68)
  Pallas kernels: 96 us -> 68 us
  local copies, waits for them, and re-layouts: 7.1 us -> 2.97 us
    pallas_call x1, Pallas kernels: 96 us -> 68 us  [body(): pl.pallas_call(functools.partial(kernel, nx, nlat, 1.0 / (4 * nx)), out_s...]
    unnamed x16 -> x4, local copies, waits for them, and re-layouts: 7.1 us -> 2.97 us
where the time goes in v2:
time: 71.9 us; the launch traced here: 71.6 us
  Pallas kernels  68 us (95%)
  local copies, waits for them, and re-layouts  2.97 us (4%)
    pallas_call x1, Pallas kernels, body(): pl.pallas_call(functools.partial(kernel, nx, nlat, 1.0 / (4 * nx)), out_s...  68 us
    unnamed x4, local copies, waits for them, and re-layouts  2.97 us

profile of v2, /device:TPU:8, one launch (start us, length us, event | category | flops | bytes accessed | tf_op | source)
XLA Modules:
  0.0 71.6 jit_solution(10630844521869024119)
XLA Ops:
  0.6 68.0 %coupled_window.1 = (f32[2,2,6,8,1536]{4,3,2,1,0:T(8,128)}, f32[6,2,192]{2,1,0:T(2,128)}) custom-call(f32[2,2,6,8,1536]{4,3,2,1,0:T(8,128)} %bitcast.5, f32[6,2,192]{2,1,0:T(2,128)} %bitcast.7, f32[6,192]{1,0:T(8,128)} %visc_hbm.1, s32[6,1536]{1,0:T(8,128)} %mask_hbm.1, s32[2]{0:T(128)} %pick_hbm.1, f32[3,32]{1,0:T(4,128)} %bitcast.9, f32[8,8]{1,0:T(8,128)} %mixing_hbm.1), custom_call_target="tpu_custom_call" | custom-call | tf_op jit(solution)/shard_map/coupled_window/pallas_call | solution.py:411
  68.6 0.0 copy-start
  68.6 2.4 %copy.11 = f32[2,2,8,6,1536]{4,2,3,1,0:T(8,128)} copy(f32[2,2,8,6,1536]{4,2,3,1,0:T(8,128)} %bitcast.6) | data formatting | bytes 2359296
  71.0 0.0 copy-done
  71.0 0.6 copy.12
Async XLA Ops:
  68.6 2.4 %copy-start = (f32[6,2,192]{2,1,0:T(2,128)S(1)}, f32[6,2,192]{2,1,0:T(2,128)}, u32[]{:S(2)}) copy-start(f32[6,2,192]{2,1,0:T(2,128)} %get-tuple-element.5) | copy-start | bytes 27652

commit v3 on v2

--- a/solution.py
+++ b/solution.py
@@ -45,9 +45,9 @@
     nx, nlat, scale,
     atm, ocean_hbm, visc_hbm, mask_hbm, pick_hbm, table_hbm, mixing_hbm, atm_out, ocean_out,
     ocean_in, visc_in, mask_in, pick, table, mixing,
-    state, coef, diff, surf, chunks, masks, ocean, visc, mask, force, part, gather_x, total, gather_y, gather_f, seg,
+    state, coef, diff, surf, chunks, masks, ocean, visc, mask, force, part, gather_r, gather_f, gather_l, seg,
     load_sem, halo_send, halo_recv, seg_send, seg_recv, pair_send, pair_recv, mask_send, mask_recv,
-    x_send, x_recv, y_send, y_recv, f_send, f_recv, out_sem, small_sem,
+    r_send, r_recv, f_send, f_recv, l_send, l_recv, small_sem,
 ):
     me = lax.axis_index("member")
     lat = lax.axis_index("lat")
@@ -57,6 +57,9 @@
     lon = mask_in.shape[1]
     pieces = lon // CHUNK
     quarter = lon // nx
+    columns = lon // LANES
+    window = quarter // LANES
+    members = 2 * nx
 
     def peers():
         for side in (-1, 0, 1):
@@ -88,9 +91,12 @@
         load.start()
 
     barrier = pltpu.get_barrier_semaphore()
-    pl.semaphore_signal(barrier, inc=1, device_id=partner, device_id_type=MESH)
+    for step in range(1, members):
+        device = (lax.rem(me + step, members), lat)
+        pl.semaphore_signal(barrier, inc=1, device_id=device, device_id_type=MESH)
     for side, step, device in peers():
-        guarded(side, lambda device=device: pl.semaphore_signal(barrier, inc=1, device_id=device, device_id_type=MESH))
+        if side:
+            guarded(side, lambda device=device: pl.semaphore_signal(barrier, inc=1, device_id=device, device_id_type=MESH))
 
     for load in small:
         load.wait()
@@ -110,22 +116,24 @@
         for b in range(6):
             state[b, 2] = row_zero
         masks[0] = jnp.zeros((8, lon), F32)
-        for a in range(2):
-            for i in range(nx):
+        gather_l[0] = jnp.zeros((window, 2, 8, LANES), F32)
+        for i in range(nx):
+            gather_f[0, i] = jnp.zeros((window, 2, 8, LANES), F32)
+            for a in range(2):
                 chunks[a, 0, i] = jnp.zeros((3, 8, 2 * LANES), F32)
-                gather_f[a, 0, i] = jnp.zeros((2, 8, quarter), F32)
 
     @pl.when(lat == nlat - 1)
     def _():
         for b in range(6):
             state[b, 9] = row_zero
         masks[2] = jnp.zeros((8, lon), F32)
-        for a in range(2):
-            for i in range(nx):
+        gather_l[2] = jnp.zeros((window, 2, 8, LANES), F32)
+        for i in range(nx):
+            gather_f[2, i] = jnp.zeros((window, 2, 8, LANES), F32)
+            for a in range(2):
                 chunks[a, 2, i] = jnp.zeros((3, 8, 2 * LANES), F32)
-                gather_f[a, 2, i] = jnp.zeros((2, 8, quarter), F32)
-
-    pl.semaphore_wait(barrier, nx + nx * has_south.astype(jnp.int32) + nx * has_north.astype(jnp.int32))
+
+    pl.semaphore_wait(barrier, members - 1 + nx * has_south.astype(jnp.int32) + nx * has_north.astype(jnp.int32))
 
     def halo(cp, side, depth):
         row = 5 - depth if side > 0 else depth
@@ -137,8 +145,8 @@
             device_id=(me, lat + side), device_id_type=MESH,
         )
 
-    def start_halos(cp):
-        for depth in range(3):
+    def start_halos(cp, depths):
+        for depth in depths:
             for side in (-1, 1):
                 guarded(side, lambda side=side, depth=depth: halo(cp, side, depth).start())
 
@@ -165,11 +173,9 @@
         )
 
     pair.start()
-    start_halos(0)
     for side, step, device in peers():
         guarded(side, lambda a=(side, step, device): spread(0, *a).start())
-    for side in (-1, 1):
-        guarded(side, lambda side=side: send_mask(side).start())
+    start_halos(0, (0, 1))
     chunks[yh, 1, x] = seg[...]
 
     sub = sublane((8, LANES))
@@ -220,7 +226,10 @@
             value = near + pltpu.roll(far, 4, 0)
             if with_surface:
                 value = value + surf[e - 1, c, m, :, off : off + CHUNK]
-            state[target, e, c, m, :, off : off + CHUNK] = value
+            if target == 6:
+                atm_out[c, m, e - 3, :, off : off + CHUNK] = value
+            else:
+                state[target, e, c, m, :, off : off + CHUNK] = value
 
     def rows(source, target, first, stride, count, with_surface):
         def body(i, carry):
@@ -255,68 +264,74 @@
         low = -depth
         rows(3 * cp, 3 * cp + 1, low, 5 - 2 * low, 2, False)
 
-    def ocean_steps(cp):
+    def advance(here, rate, sea, drive):
+        width = here.shape[1]
+        lap = (
+            pltpu.roll(here, width - 1, 1) + pltpu.roll(here, 1, 1)
+            + pltpu.roll(here, 15, 0) + pltpu.roll(here, 1, 0) - 4.0 * here
+        )
+        return here + sea * (OCEAN_GAIN * drive + rate * lap)
+
+    def ocean_steps():
         for c in range(2):
             for q in range(nx):
-                blocks = [gather_f[cp, side, q, c] for side in range(3)]
-                force[c, :, q * quarter : (q + 1) * quarter] = stack_rows(*blocks)
+                for j in range(window):
+                    blocks = [gather_f[side, q, j, c] for side in range(3)]
+                    start = q * quarter + j * LANES
+                    force[c, :, start : start + LANES] = stack_rows(*blocks)
         for _ in range(2):
             for c in range(2):
-                here = ocean[c]
-                lap = (
-                    pltpu.roll(here, lon - 1, 1) + pltpu.roll(here, 1, 1)
-                    + pltpu.roll(here, 15, 0) + pltpu.roll(here, 1, 0) - 4.0 * here
-                )
                 rate = visc[...] if c == 1 else OCEAN_DIFFUSION
-                ocean[c] = here + mask[...] * (OCEAN_GAIN * force[c] + rate * lap)
-
-    def send_x(cp, step):
-        to = lax.rem(x + step, nx)
+                ocean[c] = advance(ocean[c], rate, mask[...], force[c])
+
+    def first_tile(cp, member):
+        if cp == 0:
+            return window * lax.rem(member, nx)
+        return lax.rem(lax.div(3 * member + 2 * columns - 1, 2), columns)
+
+    def send_r(cp, step):
+        to = lax.rem(me + step, members)
         return pltpu.make_async_remote_copy(
-            part.at[cp, to], gather_x.at[cp, step - 1], x_send.at[cp, step - 1], x_recv.at[cp, step - 1],
-            device_id=(yh * nx + to, lat), device_id_type=MESH,
-        )
-
-    def send_y(cp):
+            part.at[cp, pl.ds(first_tile(cp, to), window)], gather_r.at[cp, step - 1],
+            r_send.at[cp, step - 1], r_recv.at[cp, step - 1], device_id=(to, lat), device_id_type=MESH,
+        )
+
+    def send_f(side, step, device):
         return pltpu.make_async_remote_copy(
-            total.at[cp], gather_y.at[cp], y_send.at[cp], y_recv.at[cp], device_id=partner, device_id_type=MESH
-        )
-
-    def send_f(cp, side, step, device):
+            gather_f.at[1, x], gather_f.at[1 - side, x], f_send.at[side + 1, step],
+            f_recv.at[side + 1, step], device_id=device, device_id_type=MESH,
+        )
+
+    def send_l(side):
+        k = (side + 1) // 2
         return pltpu.make_async_remote_copy(
-            gather_f.at[cp, 1, x], gather_f.at[cp, 1 - side, x], f_send.at[cp, side + 1, step],
-            f_recv.at[cp, side + 1, step], device_id=device, device_id_type=MESH,
+            gather_l.at[1], gather_l.at[1 - side], l_send.at[k], l_recv.at[k],
+            device_id=(me, lat + side), device_id_type=MESH,
         )
 
     def flux(cp):
-        last = 3 * cp + 3
-        count = lon // LANES
         for c in range(2):
-            weights = [tiles(exv[c][m], count) for m in range(2)]
+            weights = [tiles(exv[c][m], columns) for m in range(2)]
             own = pltpu.roll(ocean[c], 12, 0)[0:8]
             value = jnp.zeros((8, lon), F32)
             for row in range(6):
-                line = weights[0] * state[last, row + 3, c, 0] + weights[1] * state[last, row + 3, c, 1]
+                last = [atm_out[c, m, row] if cp else state[3, row + 3, c, m] for m in range(2)]
+                line = weights[0] * last[0] + weights[1] * last[1]
                 value = value + (pltpu.roll(line, row, 0) if row else line)
             value = value - (exc[c][0] + exc[c][1]) * own
-            for q in range(nx):
-                part[cp, q, c] = value[:, q * quarter : (q + 1) * quarter]
-
-    def stage_y(cp):
-        for step in range(1, nx):
-            send_x(cp, step).wait_recv()
-        total[cp] = (part[cp, x] + gather_x[cp, 0]) + (gather_x[cp, 1] + gather_x[cp, 2])
-        send_y(cp).start()
-
-    def stage_f(cp):
-        send_y(cp).wait_recv()
-        gather_f[cp, 1, x] = (total[cp] + gather_y[cp]) * scale
-        for side, step, device in peers():
-            guarded(side, lambda a=(side, step, device): send_f(cp, *a).start())
-
-    def wait_f(cp):
-        for side, step, device in peers():
-            guarded(-side, lambda a=(side, step, device): send_f(cp, *a).wait_recv())
+            for j in range(columns + 2):
+                start = j % columns * LANES
+                part[cp, j, c] = value[:, start : start + LANES]
+        for step in range(1, members):
+            send_r(cp, step).start()
+
+    def total(cp):
+        for step in range(1, members):
+            send_r(cp, step).wait_recv()
+        parts = [part[cp, pl.ds(first_tile(cp, me), window)]] + [gather_r[cp, k] for k in range(members - 1)]
+        while len(parts) > 1:
+            parts = [a + b for a, b in zip(parts[0::2], parts[1::2])]
+        return parts[0] * scale
 
     for load in loads:
         load.wait()
@@ -324,6 +339,9 @@
     pair.wait_recv()
     for side, step, device in peers():
         guarded(side, lambda a=(side, step, device): spread(1, *a).start())
+    start_halos(0, (2,))
+    for side in (-1, 1):
+        guarded(side, lambda side=side: send_mask(side).start())
     for depth in range(3):
         first_rows(0, depth)
     for stage in range(2):
@@ -337,56 +355,61 @@
                 odd = chunks[(2 * q + 1) // nx, side, (2 * q + 1) % nx, field]
                 blocks.append(join_chunks(even, odd))
             value = stack_rows(*blocks)
-            columns = slice(q * quarter, (q + 1) * quarter)
+            span = slice(q * quarter, (q + 1) * quarter)
             if field == 2:
-                visc[:, columns] = value
+                visc[:, span] = value
             else:
-                ocean[field, :, columns] = value
+                ocean[field, :, span] = value
     add_surface(1)
     rows(1, 2, -1, 1, 8, True)
     rows(2, 3, 0, 1, 6, True)
     flux(0)
-    for step in range(1, nx):
-        send_x(0, step).start()
-    start_halos(1)
+    start_halos(1, range(3))
     rows(3, 4, 1, 1, 4, False)
-    stage_y(0)
     first_rows(1, 0)
     first_rows(1, 1)
-    stage_f(0)
+    gather_f[1, x] = total(0)
+    for side, step, device in peers():
+        guarded(side, lambda a=(side, step, device): send_f(*a).start())
     first_rows(1, 2)
     for side in (-1, 1):
         guarded(-side, lambda side=side: send_mask(side).wait_recv())
     mask[...] = stack_rows(masks[0], masks[1], masks[2])
-    wait_f(0)
-    ocean_steps(0)
+    for side, step, device in peers():
+        guarded(-side, lambda a=(side, step, device): send_f(*a).wait_recv())
+    ocean_steps()
 
     add_surface(4)
     rows(4, 5, -1, 1, 8, True)
     rows(5, 6, 0, 1, 6, True)
     flux(1)
-    for step in range(1, nx):
-        send_x(1, step).start()
-    stores = [pltpu.make_async_copy(state.at[6, r + 3], atm_out.at[:, :, r], out_sem.at[r]) for r in range(6)]
-    for store in stores:
-        store.start()
-    stage_y(1)
-    stage_f(1)
-    wait_f(1)
-    ocean_steps(1)
-    start = pl.multiple_of(((3 * me) // 2) * LANES, LANES)
+    gather_l[1] = total(1)
+    for side in (-1, 1):
+        guarded(side, lambda side=side: send_l(side).start())
+    starts = [pl.multiple_of(lax.rem(first_tile(1, me) + j, columns) * LANES, LANES) for j in range(window)]
+
+    def windowed(ref, *lead):
+        return jnp.concatenate([ref[(*lead, slice(None), pl.ds(start, LANES))] for start in starts], axis=1)
+
+    here = [windowed(ocean, c) for c in range(2)]
+    rates = [OCEAN_DIFFUSION, windowed(visc)]
+    sea = windowed(mask)
     odd = lax.rem(me, 2) == 1
+    for side in (-1, 1):
+        guarded(-side, lambda side=side: send_l(side).wait_recv())
     for c in range(2):
-        value = ocean[c, :, pl.ds(start, 2 * LANES)]
-        value = jnp.where(odd, pltpu.roll(value, 192, 1), value)
+        drive = jnp.concatenate(
+            [stack_rows(*[gather_l[side, j, c] for side in range(3)]) for j in range(window)], axis=1
+        )
+        value = advance(advance(here[c], rates[c], sea, drive), rates[c], sea, drive)
+        value = jnp.where(odd, pltpu.roll(value, 64, 1), value)
         for r in range(6):
-            ocean_out[r, c : c + 1, :] = value[r + 4 : r + 5, 0:192]
-
-    for store in stores:
-        store.wait()
+            ocean_out[r, c : c + 1, :] = value[r + 4 : r + 5, LANES : LANES + 192]
+
     pair.wait_send()
     for side in (-1, 1):
         guarded(side, lambda side=side: send_mask(side).wait_send())
+        guarded(side, lambda side=side: send_l(side).wait_send())
         for cp in range(2):
             for depth in range(3):
                 guarded(side, lambda a=(cp, side, depth): halo(*a).wait_send())
@@ -394,18 +417,29 @@
         for side, step, device in peers():
             guarded(side, lambda a=(stage, side, step, device): spread(*a).wait_send())
     for cp in range(2):
-        send_y(cp).wait_send()
-        for step in range(1, nx):
-            send_x(cp, step).wait_send()
-        for side, step, device in peers():
-            guarded(side, lambda a=(cp, side, step, device): send_f(*a).wait_send())
+        for step in range(1, members):
+            send_r(cp, step).wait_send()
+    for side, step, device in peers():
+        guarded(side, lambda a=(side, step, device): send_f(*a).wait_send())
+
+
+def store(atm, ocean, atm_out, ocean_out, sem):
+    copies = [pltpu.make_async_copy(ocean, ocean_out, sem.at[4])]
+    copies += [pltpu.make_async_copy(atm.at[c, m], atm_out.at[c, m], sem.at[2 * c + m]) for c in range(2) for m in range(2)]
+    for copy in copies:
+        copy.start()
+    for copy in copies:
+        copy.wait()
 
 
 def body(nx, nlat, atmosphere, ocean_state, viscosity, sea_mask, parameter_index, parameter_table, level_mix):
     lon = atmosphere.shape[4]
     quarter = lon // nx
     vmem = pl.BlockSpec(memory_space=pltpu.VMEM)
-    hbm = pl.BlockSpec(memory_space=pl.ANY)
+    hbm = pl.BlockSpec(memory_space=pltpu.HBM)
+    anywhere = pl.BlockSpec(memory_space=pl.ANY)
+    window = quarter // LANES
+    members = 2 * nx
     dma = pltpu.SemaphoreType.DMA
     fields = jnp.transpose(atmosphere, (0, 1, 3, 2, 4))
     atm_out, ocean_out = pl.pallas_call(
@@ -415,7 +449,7 @@
             jax.ShapeDtypeStruct((6, 2, 192), F32),
         ),
         in_specs=[hbm] * 7,
-        out_specs=(hbm, vmem),
+        out_specs=(vmem, vmem),
         scratch_shapes=[
             pltpu.VMEM((6, 2, 192), F32),
             pltpu.VMEM((6, 192), F32),
@@ -423,7 +457,7 @@
             pltpu.SMEM((2,), jnp.int32),
             pltpu.SMEM(parameter_table.shape[::-1], F32),
             pltpu.VMEM((8, 8), F32),
-            pltpu.VMEM((7, 12, 2, 2, 8, lon), F32),
+            pltpu.VMEM((6, 12, 2, 2, 8, lon), F32),
             pltpu.VMEM((2, 2, 8, 8, LANES), F32),
             pltpu.VMEM((2, 2, 8, LANES), F32),
             pltpu.VMEM((10, 2, 2, 8, lon), F32),
@@ -433,11 +467,10 @@
             pltpu.VMEM((16, lon), F32),
             pltpu.VMEM((16, lon), F32),
             pltpu.VMEM((2, 16, lon), F32),
-            pltpu.VMEM((2, nx, 2, 8, quarter), F32),
-            pltpu.VMEM((2, nx - 1, 2, 8, quarter), F32),
-            pltpu.VMEM((2, 2, 8, quarter), F32),
-            pltpu.VMEM((2, 2, 8, quarter), F32),
-            pltpu.VMEM((2, 3, nx, 2, 8, quarter), F32),
+            pltpu.VMEM((2, lon // LANES + 2, 2, 8, LANES), F32),
+            pltpu.VMEM((2, members - 1, window, 2, 8, LANES), F32),
+            pltpu.VMEM((3, nx, window, 2, 8, LANES), F32),
+            pltpu.VMEM((3, window, 2, 8, LANES), F32),
             pltpu.VMEM((3, 8, 2 * LANES), F32),
             dma((6,)),
             dma((2, 2, 3)),
@@ -448,28 +481,41 @@
             dma(()),
             dma((2,)),
             dma((2,)),
-            dma((2, nx - 1)),
-            dma((2, nx - 1)),
+            dma((2, members - 1)),
+            dma((2, members - 1)),
+            dma((3, nx)),
+            dma((3, nx)),
             dma((2,)),
             dma((2,)),
-            dma((2, 3, nx)),
-            dma((2, 3, nx)),
-            dma((6,)),
             dma((6,)),
         ],
         compiler_params=pltpu.CompilerParams(
-            collective_id=0, has_side_effects=True, vmem_limit_bytes=67043328
+            collective_id=0, has_side_effects=True, vmem_limit_bytes=44 * 1024 * 1024
         ),
         name="coupled_window",
     )(
-        fields,
-        jnp.transpose(ocean_state, (1, 0, 2)),
-        viscosity,
-        sea_mask,
-        parameter_index,
-        jnp.transpose(parameter_table),
-        level_mix,
+        *[
+            pltpu.with_memory_space_constraint(operand, pltpu.HBM)
+            for operand in (
+                fields,
+                jnp.transpose(ocean_state, (1, 0, 2)),
+                viscosity,
+                sea_mask,
+                parameter_index,
+                jnp.transpose(parameter_table),
+                level_mix,
+            )
+        ]
     )
+    atm_out, ocean_out = pl.pallas_call(
+        store,
+        out_shape=(jax.ShapeDtypeStruct(atm_out.shape, F32), jax.ShapeDtypeStruct(ocean_out.shape, F32)),
+        in_specs=[anywhere] * 2,
+        out_specs=(hbm, hbm),
+        scratch_shapes=[dma((5,))],
+        compiler_params=pltpu.CompilerParams(vmem_limit_bytes=1024 * 1024),
+        name="store",
+    )(atm_out, ocean_out)
     return jnp.transpose(atm_out, (0, 1, 3, 2, 4)), jnp.transpose(ocean_out, (1, 0, 2))
 
 

time: 71.9 us -> 66 us (0.918)
  the two profiles are of different devices: /device:TPU:8 before, /device:TPU:14 now
where the time goes in v3:
time: 66 us; the launch traced here: 65.8 us
  Pallas kernels  65.2 us (99%)
    pallas_call x1, Pallas kernels, body(): pl.pallas_call(functools.partial(kernel, nx, nlat, 1.0 / (4 * nx)), out_s...  64.1 us

profile of v3, /device:TPU:14, one launch (start us, length us, event | category | flops | bytes accessed | tf_op | source)
XLA Modules:
  0.0 65.8 jit_solution(1053944867470779416)
XLA Ops:
  0.6 64.1 %coupled_window.1 = (f32[2,2,6,8,1536]{4,3,2,1,0:T(8,128)S(1)}, f32[6,2,192]{2,1,0:T(2,128)S(1)}) custom-call(f32[2,2,6,8,1536]{4,3,2,1,0:T(8,128)} %bitcast.5, f32[6,2,192]{2,1,0:T(2,128)} %bitcast.6, f32[6,192]{1,0:T(8,128)} %visc_hbm.1, s32[6,1536]{1,0:T(8,128)} %mask_hbm.1, s32[2]{0:T(128)} %pick_hbm.1, f32[3,32]{1,0:T(4,128)} %bitcast.7, f32[8,8]{1,0:T(8,128)} %mixing_hbm.1), custom_call_target="tpu_custom_call" | custom-call | tf_op jit(solution)/shard_map/coupled_window/pallas_call | solution.py:445
  64.8 1.1 %store.1 = (f32[2,2,6,8,1536]{4,3,2,1,0:T(8,128)}, f32[6,2,192]{2,1,0:T(2,128)}) custom-call(f32[2,2,6,8,1536]{4,3,2,1,0:T(8,128)S(1)} %get-tuple-element.6.atm, f32[6,2,192]{2,1,0:T(2,128)S(1)} %get-tuple-element.7.ocean), custom_call_target="tpu_custom_call" | custom-call | tf_op jit(solution)/shard_map/store/pallas_call | solution.py:510

commit v4 on v3

--- a/solution.py
+++ b/solution.py
@@ -26,9 +26,9 @@
 
 def stack_rows(south, own, north):
     index = sublane(own.shape)
-    middle = pltpu.roll(own, 4, 0)
-    low = jnp.where(index < 4, pltpu.roll(south, 6, 0), middle)
-    high = jnp.where(index < 2, middle, pltpu.roll(north, 2, 0))
+    middle = pltpu.roll(own, 5, 0)
+    low = jnp.where(index < 5, pltpu.roll(south, 7, 0), middle)
+    high = jnp.where(index < 3, middle, pltpu.roll(north, 3, 0))
     return jnp.concatenate([low, high], axis=0)
 
 
@@ -45,9 +45,10 @@
     nx, nlat, scale,
     atm, ocean_hbm, visc_hbm, mask_hbm, pick_hbm, table_hbm, mixing_hbm, atm_out, ocean_out,
     ocean_in, visc_in, mask_in, pick, table, mixing,
-    state, coef, diff, surf, chunks, masks, ocean, visc, mask, force, part, gather_r, gather_f, gather_l, seg,
+    state, coef, first, diff, surf, level, chunks, masks, ocean, visc, mask, force, part, gather_r, gather_f, seg,
+    raw_ocean, raw_visc,
     load_sem, halo_send, halo_recv, seg_send, seg_recv, pair_send, pair_recv, mask_send, mask_recv,
-    r_send, r_recv, f_send, f_recv, l_send, l_recv, small_sem,
+    r_send, r_recv, f_send, f_recv, small_sem,
 ):
     me = lax.axis_index("member")
     lat = lax.axis_index("lat")
@@ -75,7 +76,7 @@
         else:
             run()
 
-    loads = [pltpu.make_async_copy(atm.at[:, :, r], state.at[0, r + 3], load_sem.at[r]) for r in range(6)]
+    loads = [pltpu.make_async_copy(atm.at[:, :, r], state.at[0, r + 4], load_sem.at[r]) for r in range(6)]
     small = [
         pltpu.make_async_copy(source, target, small_sem.at[i])
         for i, (source, target) in enumerate(
@@ -98,47 +99,12 @@
         if side:
             guarded(side, lambda device=device: pl.semaphore_signal(barrier, inc=1, device_id=device, device_id_type=MESH))
 
-    for load in small:
-        load.wait()
-
-    lane_pad = jnp.zeros((8, 2 * LANES), F32)
-    for field in range(3):
-        seg[field] = lane_pad
-        for r in range(6):
-            line = visc_in[r : r + 1, :] if field == 2 else ocean_in[r, field : field + 1, :]
-            seg[field, r : r + 1, 0:192] = line
-    masks[1] = jnp.zeros((8, lon), F32)
-    masks[1, 0:6, :] = mask_in[...].astype(F32)
-    row_zero = jnp.zeros((2, 2, 8, lon), F32)
-
-    @pl.when(lat == 0)
-    def _():
-        for b in range(6):
-            state[b, 2] = row_zero
-        masks[0] = jnp.zeros((8, lon), F32)
-        gather_l[0] = jnp.zeros((window, 2, 8, LANES), F32)
-        for i in range(nx):
-            gather_f[0, i] = jnp.zeros((window, 2, 8, LANES), F32)
-            for a in range(2):
-                chunks[a, 0, i] = jnp.zeros((3, 8, 2 * LANES), F32)
-
-    @pl.when(lat == nlat - 1)
-    def _():
-        for b in range(6):
-            state[b, 9] = row_zero
-        masks[2] = jnp.zeros((8, lon), F32)
-        gather_l[2] = jnp.zeros((window, 2, 8, LANES), F32)
-        for i in range(nx):
-            gather_f[2, i] = jnp.zeros((window, 2, 8, LANES), F32)
-            for a in range(2):
-                chunks[a, 2, i] = jnp.zeros((3, 8, 2 * LANES), F32)
-
     pl.semaphore_wait(barrier, members - 1 + nx * has_south.astype(jnp.int32) + nx * has_north.astype(jnp.int32))
 
     def halo(cp, side, depth):
         row = 5 - depth if side > 0 else depth
-        there = 2 - depth if side > 0 else 9 + depth
-        source = atm.at[:, :, row] if cp == 0 else state.at[3, row + 3]
+        there = 3 - depth if side > 0 else 10 + depth
+        source = atm.at[:, :, row] if cp == 0 else state.at[3, row + 4]
         k = (side + 1) // 2
         return pltpu.make_async_remote_copy(
             source, state.at[3 * cp, there], halo_send.at[cp, k, depth], halo_recv.at[cp, k, depth],
@@ -162,9 +128,20 @@
             device_id=device, device_id_type=MESH,
         )
 
-    pair = pltpu.make_async_remote_copy(
-        seg, chunks.at[yh, 1, x], pair_send, pair_recv, device_id=partner, device_id_type=MESH
-    )
+    pairs = [
+        pltpu.make_async_remote_copy(
+            source, target, pair_send.at[k], pair_recv.at[k], device_id=partner, device_id_type=MESH
+        )
+        for k, (source, target) in enumerate(((ocean_hbm, raw_ocean), (visc_hbm, raw_visc)))
+    ]
+
+    def pack(ocean_ref, visc_ref):
+        fields = []
+        for field in range(3):
+            lines = [visc_ref[r : r + 1, :] if field == 2 else ocean_ref[r, field : field + 1, :] for r in range(6)]
+            block = jnp.concatenate(lines + [jnp.zeros((2, 192), F32)], axis=0)
+            fields.append(jnp.concatenate([block, jnp.zeros((8, 64), F32)], axis=1))
+        return jnp.stack(fields)
 
     def send_mask(side):
         return pltpu.make_async_remote_copy(
@@ -172,11 +149,41 @@
             device_id=(me, lat + side), device_id_type=MESH,
         )
 
-    pair.start()
+    for pair in pairs:
+        pair.start()
+    start_halos(0, (0, 1))
+    for load in small:
+        load.wait()
+
+    own = pack(ocean_in, visc_in)
+    seg[...] = own
+    chunks[yh, 1, x] = own
     for side, step, device in peers():
         guarded(side, lambda a=(side, step, device): spread(0, *a).start())
-    start_halos(0, (0, 1))
-    chunks[yh, 1, x] = seg[...]
+    masks[1] = jnp.zeros((8, lon), F32)
+    masks[1, 0:6, :] = mask_in[...].astype(F32)
+    row_zero = jnp.zeros((2, 2, 8, lon), F32)
+
+    @pl.when(lat == 0)
+    def _():
+        for b in range(6):
+            state[b, 3] = row_zero
+        masks[0] = jnp.zeros((8, lon), F32)
+        for i in range(nx):
+            gather_f[0, i] = jnp.zeros((window, 2, 8, LANES), F32)
+            for a in range(2):
+                chunks[a, 0, i] = jnp.zeros((3, 8, 2 * LANES), F32)
+
+    @pl.when(lat == nlat - 1)
+    def _():
+        for b in range(6):
+            state[b, 10] = row_zero
+        masks[2] = jnp.zeros((8, lon), F32)
+        for i in range(nx):
+            gather_f[2, i] = jnp.zeros((window, 2, 8, LANES), F32)
+            for a in range(2):
+                chunks[a, 2, i] = jnp.zeros((3, 8, 2 * LANES), F32)
+
 
     sub = sublane((8, LANES))
     top = sub == 0
@@ -190,6 +197,7 @@
         diff[m, 0] = jnp.full((8, LANES), dif[m], F32)
         diff[m, 1] = jnp.full((8, LANES), 1.0 - 4.0 * dif[m], F32) / diff[m, 0]
         diff[m, 0] = (0.5 * ADVECTION) / diff[m, 0]
+    level_zero = [[jnp.zeros((8, LANES), F32) for m in range(2)] for c in range(2)]
     for r in range(8):
         diagonal = jnp.sum(jnp.where(col8 == lax.rem(row8 - r + 8, 8), mix, 0.0), axis=1, keepdims=True)
         value = jnp.broadcast_to(diagonal, (8, LANES))
@@ -198,9 +206,16 @@
         for c in range(2):
             for m in range(2):
                 weight = dif[m] * jnp.where(top, value * (1.0 - exc[c][m]), value)
-                coef[c, m, r] = pltpu.roll(weight, 4, 0) if r >= 4 else weight
-
-    def unit(source, target, e, m, k, with_surface):
+                others = jnp.where(sub == r, 0.0, weight)
+                level_zero[c][m] = level_zero[c][m] + (weight - others)
+                coef[0, c, m, r] = pltpu.roll(weight, 4, 0) if r >= 4 else weight
+                coef[1, c, m, r] = pltpu.roll(others, 4, 0) if r >= 4 else others
+    for c in range(2):
+        for m in range(2):
+            first[c, m] = level_zero[c][m]
+
+    def unit(source, target, e, m, k, kind):
+        table_of = 1 if kind == 1 else 0
         width = CHUNK // LANES
         off, right, left = k * CHUNK, (k + 1) % pieces * CHUNK, (k * CHUNK - LANES) % lon
         gain = tiles(diff[m, 0], width)
@@ -217,52 +232,78 @@
             if c == 1:
                 wind = gain * centre
             advected = keep * centre + ((east + west) + (north + south)) - wind * (east - west)
-            near = tiles(coef[c, m, 0], width) * advected
-            far = tiles(coef[c, m, 4], width) * advected
+            near = tiles(coef[table_of, c, m, 0], width) * advected
+            far = tiles(coef[table_of, c, m, 4], width) * advected
             for r in range(1, 4):
                 turned = pltpu.roll(advected, r, 0)
-                near = near + tiles(coef[c, m, r], width) * turned
-                far = far + tiles(coef[c, m, r + 4], width) * turned
+                near = near + tiles(coef[table_of, c, m, r], width) * turned
+                far = far + tiles(coef[table_of, c, m, r + 4], width) * turned
             value = near + pltpu.roll(far, 4, 0)
-            if with_surface:
-                value = value + surf[e - 1, c, m, :, off : off + CHUNK]
+            if kind == 2:
+                value = value + surf[e - 3, c, m, :, off : off + CHUNK]
             if target == 6:
-                atm_out[c, m, e - 3, :, off : off + CHUNK] = value
+                atm_out[c, m, e - 4, :, off : off + CHUNK] = value
             else:
                 state[target, e, c, m, :, off : off + CHUNK] = value
 
-    def rows(source, target, first, stride, count, with_surface):
+    def rows(source, target, start, stride, count, kind):
         def body(i, carry):
-            row = first + i * stride
+            row = start + i * stride
             inside = ((row >= 0) | has_south) & ((row <= 5) | has_north)
 
             @pl.when(inside)
             def _():
                 for m in range(2):
                     for k in range(pieces):
-                        unit(source, target, row + 3, m, k, with_surface)
+                        unit(source, target, row + 4, m, k, kind)
 
             return carry
 
         lax.fori_loop(0, count, body, 0)
 
-    def add_surface(target):
-        for row in range(-2, 8):
+    def before_surface(cp, deep, between):
+        b = 3 * cp
+        for depth in range(deep):
+            if between is not None and depth == 2:
+                between()
+            wait_halo(cp, depth)
+            rows(b, b + 1, -depth, 5 + 2 * depth, 2, 0)
+            if depth == 0:
+                rows(b + 1, b + 2, 1, 1, 4, 1)
+            else:
+                rows(b + 1, b + 2, 1 - depth, 3 + 2 * depth, 2, 1)
+        for row in range(1 - deep, 5 + deep):
             for c in range(2):
-                line = jnp.broadcast_to(ocean[c, row + 4 : row + 5, :], (8, lon))
                 for m in range(2):
-                    value = tiles(exv[c][m], lon // LANES) * line
-                    surf[row + 2, c, m] = value
+                    level[c, m, row + 5 : row + 6, :] = state[b + 1, row + 4, c, m, 0:1, :]
+
+    def add_surface(cp, deep):
+        b = 3 * cp
+        for m in range(2):
+            keep, gain = tiles(diff[m, 1], columns), tiles(diff[m, 0], columns)
+            keep, gain = jnp.concatenate([keep] * 2, axis=0), jnp.concatenate([gain] * 2, axis=0)
+            wind = None
+            for c in (1, 0):
+                here = level[c, m] + exc[c][m] * ocean[c]
+                if c == 1:
+                    wind = gain * here
+                east, west = pltpu.roll(here, lon - 1, 1), pltpu.roll(here, 1, 1)
+                around = (east + west) + (pltpu.roll(here, 15, 0) + pltpu.roll(here, 1, 0))
+                level[c, m] = keep * here + around - wind * (east - west)
+        for row in range(2 - deep, 4 + deep):
+            for c in range(2):
+                line = jnp.broadcast_to(ocean[c, row + 5 : row + 6, :], (8, lon))
+                for m in range(2):
+                    value = tiles(exv[c][m], columns) * line
+                    if 3 - deep <= row < 3 + deep:
+                        surf[row + 1, c, m] = value
 
                     def run(value=value, c=c, m=m, row=row):
-                        state[target, row + 3, c, m] = state[target, row + 3, c, m] + value
+                        lowest = jnp.broadcast_to(level[c, m, row + 5 : row + 6, :], (8, lon))
+                        change = tiles(first[c, m], columns) * lowest + value
+                        state[b + 2, row + 4, c, m] = state[b + 2, row + 4, c, m] + change
 
                     guarded(-1 if row < 0 else 1 if row > 5 else 0, run)
-
-    def first_rows(cp, depth):
-        wait_halo(cp, depth)
-        low = -depth
-        rows(3 * cp, 3 * cp + 1, low, 5 - 2 * low, 2, False)
 
     def advance(here, rate, sea, drive):
         width = here.shape[1]
@@ -302,22 +343,20 @@
             f_recv.at[side + 1, step], device_id=device, device_id_type=MESH,
         )
 
-    def send_l(side):
-        k = (side + 1) // 2
-        return pltpu.make_async_remote_copy(
-            gather_l.at[1], gather_l.at[1 - side], l_send.at[k], l_recv.at[k],
-            device_id=(me, lat + side), device_id_type=MESH,
-        )
-
     def flux(cp):
         for c in range(2):
             weights = [tiles(exv[c][m], columns) for m in range(2)]
-            own = pltpu.roll(ocean[c], 12, 0)[0:8]
+            own = pltpu.roll(ocean[c], 11 + cp, 0)[0:8]
             value = jnp.zeros((8, lon), F32)
-            for row in range(6):
-                last = [atm_out[c, m, row] if cp else state[3, row + 3, c, m] for m in range(2)]
+            for row in range(-cp, 6 + cp):
+                if cp == 0:
+                    last = [state[3, row + 4, c, m] for m in range(2)]
+                elif 0 <= row < 6:
+                    last = [atm_out[c, m, row] for m in range(2)]
+                else:
+                    last = [state[0, row + 4, c, m] for m in range(2)]
                 line = weights[0] * last[0] + weights[1] * last[1]
-                value = value + (pltpu.roll(line, row, 0) if row else line)
+                value = value + (pltpu.roll(line, row + cp, 0) if row + cp else line)
             value = value - (exc[c][0] + exc[c][1]) * own
             for j in range(columns + 2):
                 start = j % columns * LANES
@@ -335,15 +374,16 @@
 
     for load in loads:
         load.wait()
-    rows(0, 1, 1, 1, 4, False)
-    pair.wait_recv()
+    rows(0, 1, 1, 1, 4, 0)
+    for pair in pairs:
+        pair.wait_recv()
+    chunks[1 - yh, 1, x] = pack(raw_ocean, raw_visc)
     for side, step, device in peers():
         guarded(side, lambda a=(side, step, device): spread(1, *a).start())
     start_halos(0, (2,))
     for side in (-1, 1):
         guarded(side, lambda side=side: send_mask(side).start())
-    for depth in range(3):
-        first_rows(0, depth)
+    before_surface(0, 3, None)
     for stage in range(2):
         for side, step, device in peers():
             guarded(-side, lambda a=(stage, side, step, device): spread(*a).wait_recv())
@@ -360,18 +400,18 @@
                 visc[:, span] = value
             else:
                 ocean[field, :, span] = value
-    add_surface(1)
-    rows(1, 2, -1, 1, 8, True)
-    rows(2, 3, 0, 1, 6, True)
+    add_surface(0, 3)
+    rows(2, 3, 0, 1, 6, 2)
     flux(0)
-    start_halos(1, range(3))
-    rows(3, 4, 1, 1, 4, False)
-    first_rows(1, 0)
-    first_rows(1, 1)
-    gather_f[1, x] = total(0)
-    for side, step, device in peers():
-        guarded(side, lambda a=(side, step, device): send_f(*a).start())
-    first_rows(1, 2)
+    start_halos(1, range(4))
+    rows(3, 4, 1, 1, 4, 0)
+
+    def broadcast():
+        gather_f[1, x] = total(0)
+        for side, step, device in peers():
+            guarded(side, lambda a=(side, step, device): send_f(*a).start())
+
+    before_surface(1, 4, broadcast)
     for side in (-1, 1):
         guarded(-side, lambda side=side: send_mask(side).wait_recv())
     mask[...] = stack_rows(masks[0], masks[1], masks[2])
@@ -379,13 +419,10 @@
         guarded(-side, lambda a=(side, step, device): send_f(*a).wait_recv())
     ocean_steps()
 
-    add_surface(4)
-    rows(4, 5, -1, 1, 8, True)
-    rows(5, 6, 0, 1, 6, True)
+    add_surface(1, 4)
+    rows(5, 0, -1, 7, 2, 2)
+    rows(5, 6, 0, 1, 6, 2)
     flux(1)
-    gather_l[1] = total(1)
-    for side in (-1, 1):
-        guarded(side, lambda side=side: send_l(side).start())
     starts = [pl.multiple_of(lax.rem(first_tile(1, me) + j, columns) * LANES, LANES) for j in range(window)]
 
     def windowed(ref, *lead):
@@ -395,23 +432,20 @@
     rates = [OCEAN_DIFFUSION, windowed(visc)]
     sea = windowed(mask)
     odd = lax.rem(me, 2) == 1
-    for side in (-1, 1):
-        guarded(-side, lambda side=side: send_l(side).wait_recv())
+    final = total(1)
     for c in range(2):
-        drive = jnp.concatenate(
-            [stack_rows(*[gather_l[side, j, c] for side in range(3)]) for j in range(window)], axis=1
-        )
+        drive = jnp.concatenate([jnp.concatenate([pltpu.roll(final[j, c], 4, 0)] * 2, axis=0) for j in range(window)], axis=1)
         value = advance(advance(here[c], rates[c], sea, drive), rates[c], sea, drive)
         value = jnp.where(odd, pltpu.roll(value, 64, 1), value)
         for r in range(6):
-            ocean_out[r, c : c + 1, :] = value[r + 4 : r + 5, LANES : LANES + 192]
-
-    pair.wait_send()
+            ocean_out[r, c : c + 1, :] = value[r + 5 : r + 6, LANES : LANES + 192]
+
+    for pair in pairs:
+        pair.wait_send()
     for side in (-1, 1):
         guarded(side, lambda side=side: send_mask(side).wait_send())
-        guarded(side, lambda side=side: send_l(side).wait_send())
         for cp in range(2):
-            for depth in range(3):
+            for depth in range(3 + cp):
                 guarded(side, lambda a=(cp, side, depth): halo(*a).wait_send())
     for stage in range(2):
         for side, step, device in peers():
@@ -457,10 +491,12 @@
             pltpu.SMEM((2,), jnp.int32),
             pltpu.SMEM(parameter_table.shape[::-1], F32),
             pltpu.VMEM((8, 8), F32),
-            pltpu.VMEM((6, 12, 2, 2, 8, lon), F32),
-            pltpu.VMEM((2, 2, 8, 8, LANES), F32),
+            pltpu.VMEM((6, 14, 2, 2, 8, lon), F32),
+            pltpu.VMEM((2, 2, 2, 8, 8, LANES), F32),
             pltpu.VMEM((2, 2, 8, LANES), F32),
-            pltpu.VMEM((10, 2, 2, 8, lon), F32),
+            pltpu.VMEM((2, 2, 8, LANES), F32),
+            pltpu.VMEM((8, 2, 2, 8, lon), F32),
+            pltpu.VMEM((2, 2, 16, lon), F32),
             pltpu.VMEM((2, 3, nx, 3, 8, 2 * LANES), F32),
             pltpu.VMEM((3, 8, lon), F32),
             pltpu.VMEM((2, 16, lon), F32),
@@ -470,23 +506,22 @@
             pltpu.VMEM((2, lon // LANES + 2, 2, 8, LANES), F32),
             pltpu.VMEM((2, members - 1, window, 2, 8, LANES), F32),
             pltpu.VMEM((3, nx, window, 2, 8, LANES), F32),
-            pltpu.VMEM((3, window, 2, 8, LANES), F32),
             pltpu.VMEM((3, 8, 2 * LANES), F32),
+            pltpu.VMEM((6, 2, 192), F32),
+            pltpu.VMEM((6, 192), F32),
             dma((6,)),
-            dma((2, 2, 3)),
-            dma((2, 2, 3)),
+            dma((2, 2, 4)),
+            dma((2, 2, 4)),
             dma((2, 3, nx)),
             dma((2, 3, nx)),
-            dma(()),
-            dma(()),
+            dma((2,)),
+            dma((2,)),
             dma((2,)),
             dma((2,)),
             dma((2, members - 1)),
             dma((2, members - 1)),
             dma((3, nx)),
             dma((3, nx)),
-            dma((2,)),
-            dma((2,)),
             dma((6,)),
         ],
         compiler_params=pltpu.CompilerParams(

time: 66 us -> 61.4 us (0.930)
  the two profiles are of different devices: /device:TPU:14 before, /device:TPU:8 now
where the time goes in v4:
time: 61.4 us; the launch traced here: 61.3 us
  Pallas kernels  60.7 us (99%)
  between operations  0.64 us (1%)
    pallas_call x1, Pallas kernels, body(): pl.pallas_call(functools.partial(kernel, nx, nlat, 1.0 / (4 * nx)), out_s...  59.6 us

profile of v4, /device:TPU:8, one launch (start us, length us, event | category | flops | bytes accessed | tf_op | source)
XLA Modules:
  0.0 61.3 jit_solution(7359581766489246848)
XLA Ops:
  0.6 59.6 %coupled_window.1 = (f32[2,2,6,8,1536]{4,3,2,1,0:T(8,128)S(1)}, f32[6,2,192]{2,1,0:T(2,128)S(1)}) custom-call(f32[2,2,6,8,1536]{4,3,2,1,0:T(8,128)} %bitcast.5, f32[6,2,192]{2,1,0:T(2,128)} %bitcast.6, f32[6,192]{1,0:T(8,128)} %visc_hbm.1, s32[6,1536]{1,0:T(8,128)} %mask_hbm.1, s32[2]{0:T(128)} %pick_hbm.1, f32[3,32]{1,0:T(4,128)} %bitcast.7, f32[8,8]{1,0:T(8,128)} %mixing_hbm.1), custom_call_target="tpu_custom_call" | custom-call | tf_op jit(solution)/shard_map/coupled_window/pallas_call | solution.py:479
  60.2 1.1 %store.1 = (f32[2,2,6,8,1536]{4,3,2,1,0:T(8,128)}, f32[6,2,192]{2,1,0:T(2,128)}) custom-call(f32[2,2,6,8,1536]{4,3,2,1,0:T(8,128)S(1)} %get-tuple-element.6.atm, f32[6,2,192]{2,1,0:T(2,128)S(1)} %get-tuple-element.7.ocean), custom_call_target="tpu_custom_call" | custom-call | tf_op jit(solution)/shard_map/store/pallas_call | solution.py:545

commit v5 on v4

--- a/solution.py
+++ b/solution.py
@@ -46,7 +46,7 @@
     atm, ocean_hbm, visc_hbm, mask_hbm, pick_hbm, table_hbm, mixing_hbm, atm_out, ocean_out,
     ocean_in, visc_in, mask_in, pick, table, mixing,
     state, coef, first, diff, surf, level, chunks, masks, ocean, visc, mask, force, part, gather_r, gather_f, seg,
-    raw_ocean, raw_visc,
+    raw_ocean, raw_visc, bottom, tally,
     load_sem, halo_send, halo_recv, seg_send, seg_recv, pair_send, pair_recv, mask_send, mask_recv,
     r_send, r_recv, f_send, f_recv, small_sem,
 ):
@@ -210,12 +210,15 @@
                 level_zero[c][m] = level_zero[c][m] + (weight - others)
                 coef[0, c, m, r] = pltpu.roll(weight, 4, 0) if r >= 4 else weight
                 coef[1, c, m, r] = pltpu.roll(others, 4, 0) if r >= 4 else others
+    upper = jnp.sum(jnp.where(row8 == col8, jnp.broadcast_to(mix[0:1, :], (8, 8)), 0.0), axis=1, keepdims=True)
+    upper = jnp.broadcast_to(upper, (8, LANES)) + jnp.where(top, 1.0, 0.0)
+    share = [[exc[c][m] * (1.0 - exc[c][m]) for m in range(2)] for c in range(2)]
     for c in range(2):
         for m in range(2):
             first[c, m] = level_zero[c][m]
-
-    def unit(source, target, e, m, k, kind):
-        table_of = 1 if kind == 1 else 0
+            bottom[c, m] = (share[c][m] * dif[m]) * upper
+
+    def stencil(source, e, m, k):
         width = CHUNK // LANES
         off, right, left = k * CHUNK, (k + 1) % pieces * CHUNK, (k * CHUNK - LANES) % lon
         gain = tiles(diff[m, 0], width)
@@ -231,35 +234,70 @@
             west = pltpu.roll(jnp.concatenate([centre, behind], axis=1), 1, 1)[:, :CHUNK]
             if c == 1:
                 wind = gain * centre
-            advected = keep * centre + ((east + west) + (north + south)) - wind * (east - west)
-            near = tiles(coef[table_of, c, m, 0], width) * advected
-            far = tiles(coef[table_of, c, m, 4], width) * advected
-            for r in range(1, 4):
-                turned = pltpu.roll(advected, r, 0)
-                near = near + tiles(coef[table_of, c, m, r], width) * turned
-                far = far + tiles(coef[table_of, c, m, r + 4], width) * turned
-            value = near + pltpu.roll(far, 4, 0)
-            if kind == 2:
-                value = value + surf[e - 3, c, m, :, off : off + CHUNK]
-            if target == 6:
-                atm_out[c, m, e - 4, :, off : off + CHUNK] = value
-            else:
-                state[target, e, c, m, :, off : off + CHUNK] = value
-
-    def rows(source, target, start, stride, count, kind):
+            yield c, keep * centre + ((east + west) + (north + south)) - wind * (east - west)
+
+    def mixed(advected, kind, c, m):
+        width = CHUNK // LANES
+        near = tiles(coef[kind, c, m, 0], width) * advected
+        far = tiles(coef[kind, c, m, 4], width) * advected
+        for r in range(1, 4):
+            turned = pltpu.roll(advected, r, 0)
+            near = near + tiles(coef[kind, c, m, r], width) * turned
+            far = far + tiles(coef[kind, c, m, r + 4], width) * turned
+        return near + pltpu.roll(far, 4, 0)
+
+    def each_row(start, stride, count, run):
         def body(i, carry):
             row = start + i * stride
             inside = ((row >= 0) | has_south) & ((row <= 5) | has_north)
-
-            @pl.when(inside)
-            def _():
+            pl.when(inside)(lambda: run(row))
+            return carry
+
+        lax.fori_loop(0, count, body, 0)
+
+    def rows(source, target, start, stride, count, kind):
+        def run(row):
+            for m in range(2):
+                for k in range(pieces):
+                    for c, advected in stencil(source, row + 4, m, k):
+                        state[target, row + 4, c, m, :, k * CHUNK : (k + 1) * CHUNK] = mixed(advected, kind, c, m)
+
+        each_row(start, stride, count, run)
+
+    def last_rows(source, target, start, count, shift):
+        index = sublane((8, CHUNK))
+
+        def run(row):
+            for k in range(pieces):
+                span = slice(k * CHUNK, (k + 1) * CHUNK)
+                sums = [None, None]
                 for m in range(2):
-                    for k in range(pieces):
-                        unit(source, target, row + 4, m, k, kind)
-
-            return carry
-
-        lax.fori_loop(0, count, body, 0)
+                    for c, advected in stencil(source, row + 4, m, k):
+                        state[target, row + 4, c, m, :, span] = advected
+                        term = tiles(bottom[c, m], CHUNK // LANES) * advected
+                        sums[c] = term if sums[c] is None else sums[c] + term
+                for c in range(2):
+                    for turn in (4, 2, 1):
+                        sums[c] = sums[c] + pltpu.roll(sums[c], turn, 0)
+                    tally[c, :, span] = jnp.where(index == row + shift, sums[c], tally[c, :, span])
+
+        for c in range(2):
+            tally[c] = jnp.zeros((8, lon), F32)
+        each_row(start, 1, count, run)
+
+    def mix_rows(source, start, stride, count):
+        def run(row):
+            for m in range(2):
+                for k in range(pieces):
+                    span = slice(k * CHUNK, (k + 1) * CHUNK)
+                    for c in range(2):
+                        value = mixed(state[source, row + 4, c, m, :, span], 0, c, m) + surf[row + 1, c, m, :, span]
+                        if source == 3:
+                            state[3, row + 4, c, m, :, span] = value
+                        else:
+                            atm_out[c, m, row, :, span] = value
+
+        each_row(start, stride, count, run)
 
     def before_surface(cp, deep, between):
         b = 3 * cp
@@ -345,19 +383,8 @@
 
     def flux(cp):
         for c in range(2):
-            weights = [tiles(exv[c][m], columns) for m in range(2)]
             own = pltpu.roll(ocean[c], 11 + cp, 0)[0:8]
-            value = jnp.zeros((8, lon), F32)
-            for row in range(-cp, 6 + cp):
-                if cp == 0:
-                    last = [state[3, row + 4, c, m] for m in range(2)]
-                elif 0 <= row < 6:
-                    last = [atm_out[c, m, row] for m in range(2)]
-                else:
-                    last = [state[0, row + 4, c, m] for m in range(2)]
-                line = weights[0] * last[0] + weights[1] * last[1]
-                value = value + (pltpu.roll(line, row + cp, 0) if row + cp else line)
-            value = value - (exc[c][0] + exc[c][1]) * own
+            value = tally[c] - (share[c][0] + share[c][1]) * own
             for j in range(columns + 2):
                 start = j % columns * LANES
                 part[cp, j, c] = value[:, start : start + LANES]
@@ -401,9 +428,14 @@
             else:
                 ocean[field, :, span] = value
     add_surface(0, 3)
-    rows(2, 3, 0, 1, 6, 2)
+    last_rows(2, 3, 0, 6, 0)
     flux(0)
-    start_halos(1, range(4))
+    mix_rows(3, 0, 5, 2)
+    start_halos(1, (0,))
+    mix_rows(3, 1, 3, 2)
+    start_halos(1, (1,))
+    mix_rows(3, 2, 1, 2)
+    start_halos(1, (2, 3))
     rows(3, 4, 1, 1, 4, 0)
 
     def broadcast():
@@ -420,9 +452,9 @@
     ocean_steps()
 
     add_surface(1, 4)
-    rows(5, 0, -1, 7, 2, 2)
-    rows(5, 6, 0, 1, 6, 2)
+    last_rows(5, 0, -1, 8, 1)
     flux(1)
+    mix_rows(0, 0, 1, 6)
     starts = [pl.multiple_of(lax.rem(first_tile(1, me) + j, columns) * LANES, LANES) for j in range(window)]
 
     def windowed(ref, *lead):
@@ -509,6 +541,8 @@
             pltpu.VMEM((3, 8, 2 * LANES), F32),
             pltpu.VMEM((6, 2, 192), F32),
             pltpu.VMEM((6, 192), F32),
+            pltpu.VMEM((2, 2, 8, LANES), F32),
+            pltpu.VMEM((2, 8, lon), F32),
             dma((6,)),
             dma((2, 2, 4)),
             dma((2, 2, 4)),

time: 61.4 us -> 60.4 us (0.984)
  Pallas kernels: 60.7 us -> 59.6 us
    pallas_call x1, Pallas kernels: 59.6 us -> 58.6 us  [body(): pl.pallas_call(functools.partial(kernel, nx, nlat, 1.0 / (4 * nx)), out_s...]
where the time goes in v5:
time: 60.4 us; the launch traced here: 60.3 us
  Pallas kernels  59.6 us (99%)
  between operations  0.64 us (1%)
    pallas_call x1, Pallas kernels, body(): pl.pallas_call(functools.partial(kernel, nx, nlat, 1.0 / (4 * nx)), out_s...  58.6 us

profile of v5, /device:TPU:8, one launch (start us, length us, event | category | flops | bytes accessed | tf_op | source)
XLA Modules:
  0.0 60.3 jit_solution(3378130378062617454)
XLA Ops:
  0.6 58.6 %coupled_window.1 = (f32[2,2,6,8,1536]{4,3,2,1,0:T(8,128)S(1)}, f32[6,2,192]{2,1,0:T(2,128)S(1)}) custom-call(f32[2,2,6,8,1536]{4,3,2,1,0:T(8,128)} %bitcast.5, f32[6,2,192]{2,1,0:T(2,128)} %bitcast.6, f32[6,192]{1,0:T(8,128)} %visc_hbm.1, s32[6,1536]{1,0:T(8,128)} %mask_hbm.1, s32[2]{0:T(128)} %pick_hbm.1, f32[3,32]{1,0:T(4,128)} %bitcast.7, f32[8,8]{1,0:T(8,128)} %mixing_hbm.1), custom_call_target="tpu_custom_call" | custom-call | tf_op jit(solution)/shard_map/coupled_window/pallas_call | solution.py:511
  59.2 1.1 %store.1 = (f32[2,2,6,8,1536]{4,3,2,1,0:T(8,128)}, f32[6,2,192]{2,1,0:T(2,128)}) custom-call(f32[2,2,6,8,1536]{4,3,2,1,0:T(8,128)S(1)} %get-tuple-element.6.atm, f32[6,2,192]{2,1,0:T(2,128)S(1)} %get-tuple-element.7.ocean), custom_call_target="tpu_custom_call" | custom-call | tf_op jit(solution)/shard_map/store/pallas_call | solution.py:579

commit v6 on v5

--- a/solution.py
+++ b/solution.py
@@ -63,8 +63,8 @@
     members = 2 * nx
 
     def peers():
-        for side in (-1, 0, 1):
-            for step in range(nx):
+        for side in (-1, 1, 0):
+            for step in (2, 1, 3, 0):
                 if side or step:
                     yield side, step, (yh * nx + lax.rem(x + step, nx), lat + side)
 
@@ -151,7 +151,7 @@
 
     for pair in pairs:
         pair.start()
-    start_halos(0, (0, 1))
+    start_halos(0, (0, 1, 2))
     for load in small:
         load.wait()
 
@@ -302,7 +302,7 @@
     def before_surface(cp, deep, between):
         b = 3 * cp
         for depth in range(deep):
-            if between is not None and depth == 2:
+            if between is not None and depth == 0:
                 between()
             wait_halo(cp, depth)
             rows(b, b + 1, -depth, 5 + 2 * depth, 2, 0)
@@ -388,7 +388,7 @@
             for j in range(columns + 2):
                 start = j % columns * LANES
                 part[cp, j, c] = value[:, start : start + LANES]
-        for step in range(1, members):
+        for step in (2, 6, 3, 5, 4, 1, 7):
             send_r(cp, step).start()
 
     def total(cp):
@@ -407,7 +407,6 @@
     chunks[1 - yh, 1, x] = pack(raw_ocean, raw_visc)
     for side, step, device in peers():
         guarded(side, lambda a=(side, step, device): spread(1, *a).start())
-    start_halos(0, (2,))
     for side in (-1, 1):
         guarded(side, lambda side=side: send_mask(side).start())
     before_surface(0, 3, None)

time: 60.4 us -> 59.6 us (0.987)
  Pallas kernels: 59.6 us -> 58.9 us
    pallas_call x1, Pallas kernels: 58.6 us -> 57.8 us  [body(): pl.pallas_call(functools.partial(kernel, nx, nlat, 1.0 / (4 * nx)), out_s...]
where the time goes in v6:
time: 59.6 us; the launch traced here: 59.5 us
  Pallas kernels  58.9 us (99%)
  between operations  0.64 us (1%)
    pallas_call x1, Pallas kernels, body(): pl.pallas_call(functools.partial(kernel, nx, nlat, 1.0 / (4 * nx)), out_s...  57.8 us

profile of v6, /device:TPU:8, one launch (start us, length us, event | category | flops | bytes accessed | tf_op | source)
XLA Modules:
  0.0 59.5 jit_solution(2150591124919720868)
XLA Ops:
  0.6 57.8 %coupled_window.1 = (f32[2,2,6,8,1536]{4,3,2,1,0:T(8,128)S(1)}, f32[6,2,192]{2,1,0:T(2,128)S(1)}) custom-call(f32[2,2,6,8,1536]{4,3,2,1,0:T(8,128)} %bitcast.5, f32[6,2,192]{2,1,0:T(2,128)} %bitcast.6, f32[6,192]{1,0:T(8,128)} %visc_hbm.1, s32[6,1536]{1,0:T(8,128)} %mask_hbm.1, s32[2]{0:T(128)} %pick_hbm.1, f32[3,32]{1,0:T(4,128)} %bitcast.7, f32[8,8]{1,0:T(8,128)} %mixing_hbm.1), custom_call_target="tpu_custom_call" | custom-call | tf_op jit(solution)/shard_map/coupled_window/pallas_call | solution.py:510
  58.5 1.1 %store.1 = (f32[2,2,6,8,1536]{4,3,2,1,0:T(8,128)}, f32[6,2,192]{2,1,0:T(2,128)}) custom-call(f32[2,2,6,8,1536]{4,3,2,1,0:T(8,128)S(1)} %get-tuple-element.6.atm, f32[6,2,192]{2,1,0:T(2,128)S(1)} %get-tuple-element.7.ocean), custom_call_target="tpu_custom_call" | custom-call | tf_op jit(solution)/shard_map/store/pallas_call | solution.py:578

commit v7 on v6

--- a/solution.py
+++ b/solution.py
@@ -302,7 +302,7 @@
     def before_surface(cp, deep, between):
         b = 3 * cp
         for depth in range(deep):
-            if between is not None and depth == 0:
+            if depth == (0 if cp else 2):
                 between()
             wait_halo(cp, depth)
             rows(b, b + 1, -depth, 5 + 2 * depth, 2, 0)
@@ -409,23 +409,26 @@
         guarded(side, lambda a=(side, step, device): spread(1, *a).start())
     for side in (-1, 1):
         guarded(side, lambda side=side: send_mask(side).start())
-    before_surface(0, 3, None)
-    for stage in range(2):
-        for side, step, device in peers():
-            guarded(-side, lambda a=(stage, side, step, device): spread(*a).wait_recv())
-    for field in range(3):
-        for q in range(nx):
-            blocks = []
-            for side in range(3):
-                even = chunks[(2 * q) // nx, side, (2 * q) % nx, field]
-                odd = chunks[(2 * q + 1) // nx, side, (2 * q + 1) % nx, field]
-                blocks.append(join_chunks(even, odd))
-            value = stack_rows(*blocks)
-            span = slice(q * quarter, (q + 1) * quarter)
-            if field == 2:
-                visc[:, span] = value
-            else:
-                ocean[field, :, span] = value
+
+    def assemble():
+        for stage in range(2):
+            for side, step, device in peers():
+                guarded(-side, lambda a=(stage, side, step, device): spread(*a).wait_recv())
+        for field in range(3):
+            for q in range(nx):
+                blocks = []
+                for side in range(3):
+                    even = chunks[(2 * q) // nx, side, (2 * q) % nx, field]
+                    odd = chunks[(2 * q + 1) // nx, side, (2 * q + 1) % nx, field]
+                    blocks.append(join_chunks(even, odd))
+                value = stack_rows(*blocks)
+                span = slice(q * quarter, (q + 1) * quarter)
+                if field == 2:
+                    visc[:, span] = value
+                else:
+                    ocean[field, :, span] = value
+
+    before_surface(0, 3, assemble)
     add_surface(0, 3)
     last_rows(2, 3, 0, 6, 0)
     flux(0)

time: 59.6 us -> 60.8 us (1.020)
  Pallas kernels: 58.9 us -> 60 us
    pallas_call x1, Pallas kernels: 57.8 us -> 59 us  [body(): pl.pallas_call(functools.partial(kernel, nx, nlat, 1.0 / (4 * nx)), out_s...]
where the time goes in v7:
time: 60.8 us; the launch traced here: 60.7 us
  Pallas kernels  60 us (99%)
  between operations  0.64 us (1%)
    pallas_call x1, Pallas kernels, body(): pl.pallas_call(functools.partial(kernel, nx, nlat, 1.0 / (4 * nx)), out_s...  59 us

profile of v7, /device:TPU:8, one launch (start us, length us, event | category | flops | bytes accessed | tf_op | source)
XLA Modules:
  0.0 60.7 jit_solution(11410923206378311511)
XLA Ops:
  0.6 59.0 %coupled_window.1 = (f32[2,2,6,8,1536]{4,3,2,1,0:T(8,128)S(1)}, f32[6,2,192]{2,1,0:T(2,128)S(1)}) custom-call(f32[2,2,6,8,1536]{4,3,2,1,0:T(8,128)} %bitcast.5, f32[6,2,192]{2,1,0:T(2,128)} %bitcast.6, f32[6,192]{1,0:T(8,128)} %visc_hbm.1, s32[6,1536]{1,0:T(8,128)} %mask_hbm.1, s32[2]{0:T(128)} %pick_hbm.1, f32[3,32]{1,0:T(4,128)} %bitcast.7, f32[8,8]{1,0:T(8,128)} %mixing_hbm.1), custom_call_target="tpu_custom_call" | custom-call | tf_op jit(solution)/shard_map/coupled_window/pallas_call | solution.py:513
  59.6 1.1 %store.1 = (f32[2,2,6,8,1536]{4,3,2,1,0:T(8,128)}, f32[6,2,192]{2,1,0:T(2,128)}) custom-call(f32[2,2,6,8,1536]{4,3,2,1,0:T(8,128)S(1)} %get-tuple-element.6.atm, f32[6,2,192]{2,1,0:T(2,128)S(1)} %get-tuple-element.7.ocean), custom_call_target="tpu_custom_call" | custom-call | tf_op jit(solution)/shard_map/store/pallas_call | solution.py:581
